TPU v7x, 128 devices: a whole 4x4x4 slice. The times are simulated.
128 devices in a mesh: region: 16 (over y_lo, z, core), group: 8 (over y_hi, x).
Axes of the slice: x: 4, y: 4 (y_hi: 2, y_lo: 2; y = y_hi * 2 + y_lo), z: 4, core: 2. Of those that a mesh axis runs over, the one named last changes fastest.
Arguments:
- object_slab: float32 [8192, 2, 4096], P('region', None, 'group'), may hold values from -6 to 6
- probe: float32 [4, 2, 256, 256], replicated, may hold values from -6 to 6
- diffraction: float32 [512, 256, 256], P(('region', 'group')), may hold values from 0.25 to 16
- positions: int32 [512, 2], P(('region', 'group')), may hold values from 0 to 7936, as said below
- slot_counts: int32 [8, 16], P('group', 'region'), may hold values from 1 to 4, 40 in all within a row
Outputs:
- new_object: float32 [8192, 2, 4096], P('region', None, 'group')
- new_probe: float32 [4, 2, 256, 256], replicated
Inputs may be any that keep to these rules, and one draw needn't show every extreme that they name: `positions`: A slot of region index r has its row in r * 512 to min(r * 512 + 511, 7936); columns lie in 0 to 256; rows 0 and 7936 and columns 0 and 256 are each taken by some slot.
All inputs are finite; a program needn't handle non-finite values. No bound on the sum of `slot_counts` on one device may be relied on, other than what follows from the above.
Results may differ from a plain program's by a relative error of at most 0.0003.
Values sent between devices are 32-bit elements; how exact they have to be, the bound alone decides.
A program may use at most 128 MiB of HBM per device.

v0:
```python
import math

import jax
import jax.numpy as jnp
from jax import lax
from jax.sharding import PartitionSpec as P

highest = lax.Precision.HIGHEST


def shifted(block, axis, distance):
    devices = range(lax.axis_size(axis))
    route = [(i - distance, i) for i in devices if i - distance in devices]
    return lax.ppermute(block, axis, route)


def tables(side):
    index = jnp.arange(side, dtype=jnp.int32)
    prod = index[:, None] * index[None, :] % side
    angle = prod.astype(jnp.float32) * (2.0 * math.pi / side)
    scale = 1.0 / math.sqrt(side)
    return (jnp.cos(angle) * scale, -jnp.sin(angle) * scale)


def transform(real_part, imag_part, cos_tab, sin_tab):
    left_r = jnp.einsum("jk,mkl->mjl", cos_tab, real_part, precision=highest) - jnp.einsum(
        "jk,mkl->mjl", sin_tab, imag_part, precision=highest
    )
    left_i = jnp.einsum("jk,mkl->mjl", cos_tab, imag_part, precision=highest) + jnp.einsum(
        "jk,mkl->mjl", sin_tab, real_part, precision=highest
    )
    out_r = jnp.einsum("mjk,kl->mjl", left_r, cos_tab, precision=highest) - jnp.einsum(
        "mjk,kl->mjl", left_i, sin_tab, precision=highest
    )
    out_i = jnp.einsum("mjk,kl->mjl", left_r, sin_tab, precision=highest) + jnp.einsum(
        "mjk,kl->mjl", left_i, cos_tab, precision=highest
    )
    return (out_r, out_i)


def on_device(object_slab, probe, diffraction, positions, slot_counts):
    side = probe.shape[2]
    slots = diffraction.shape[0]
    tile_rows = object_slab.shape[0]
    active_count = slot_counts[0, 0]
    cos_tab, sin_tab = tables(side)
    base = lax.axis_index("region") * tile_rows
    local_rows = positions[:, 0] - base
    shard_columns = positions[:, 1]
    obj = object_slab
    prb = probe
    peak = jnp.max(jnp.sum(prb[:, 0] * prb[:, 0] + prb[:, 1] * prb[:, 1], axis=0))
    below = shifted(obj, "region", -1)
    extended = jnp.concatenate([obj, below], axis=0)

    def cut(row, col):
        return lax.dynamic_slice(extended, (row, jnp.int32(0), col), (side, 2, side))

    windows = jax.vmap(cut)(local_rows, shard_columns)
    probe_r = prb[:, 0]
    probe_i = prb[:, 1]

    def single_position(position_entry, carry):
        wgrads, pgrad, cover = carry
        live = (position_entry < active_count).astype(jnp.float32)
        win = lax.dynamic_index_in_dim(windows, position_entry, 0, keepdims=False)
        observed_intensity = lax.dynamic_index_in_dim(
            diffraction, position_entry, 0, keepdims=False
        )
        win_r = win[:, 0, :]
        win_i = win[:, 1, :]
        exit_r = probe_r * win_r[None] - probe_i * win_i[None]
        exit_i = probe_r * win_i[None] + probe_i * win_r[None]
        far_r, far_i = transform(exit_r, exit_i, cos_tab, sin_tab)
        model_intensity = jnp.sum(far_r * far_r + far_i * far_i, axis=0)
        update_ratio = 1.0 - jnp.sqrt(observed_intensity) / jnp.sqrt(
            jnp.maximum(model_intensity, 1.0)
        )
        chi_r, chi_i = transform(
            far_r * update_ratio[None], far_i * update_ratio[None], cos_tab, -sin_tab
        )
        chi_r = chi_r * live
        chi_i = chi_i * live
        go_r = jnp.sum(probe_r * chi_r + probe_i * chi_i, axis=0)
        go_i = jnp.sum(probe_r * chi_i - probe_i * chi_r, axis=0)
        grad_win = jnp.stack([go_r, go_i], axis=1)
        wgrads = lax.dynamic_update_index_in_dim(wgrads, grad_win, position_entry, 0)
        gp = jnp.stack(
            [win_r[None] * chi_r + win_i[None] * chi_i, win_r[None] * chi_i - win_i[None] * chi_r],
            axis=1,
        )
        return (wgrads, pgrad + gp, cover + live * (win_r * win_r + win_i * win_i))

    start_carry = (
        jnp.zeros((slots, side, 2, side), jnp.float32),
        jnp.zeros(prb.shape, jnp.float32),
        jnp.zeros((side, side), jnp.float32),
    )
    wgrads, pgrad, cover = lax.fori_loop(0, slots, single_position, start_carry)
    pgrad, cover = lax.psum((pgrad, cover), ("region", "group"))

    def put(position_entry, scratch_array):
        row = local_rows[position_entry]
        col = shard_columns[position_entry]
        current = lax.dynamic_slice(scratch_array, (row, jnp.int32(0), col), (side, 2, side))
        return lax.dynamic_update_slice(
            scratch_array, current + wgrads[position_entry], (row, jnp.int32(0), col)
        )

    scratch_array = lax.fori_loop(0, slots, put, jnp.zeros(extended.shape, jnp.float32))
    tile_grad = scratch_array[:tile_rows]
    spill = scratch_array[tile_rows:]
    arrived = shifted(spill, "region", 1)
    tile_grad = tile_grad + arrived
    obj = obj - tile_grad / peak
    prb = prb - pgrad / (cover + 1e-06)[None, None]
    return (obj, prb)


def solution(mesh):
    placed = (
        P("region", None, "group"),
        P(),
        P(("region", "group"), None, None),
        P(("region", "group"), None),
        P("group", "region"),
    )
    return jax.shard_map(
        on_device,
        mesh=mesh,
        in_specs=placed,
        out_specs=(P("region", None, "group"), P()),
        check_vma=False,
    )
```

profile of v0, /device:TPU:1, one launch (start us, length us, event | category | flops | bytes accessed | tf_op | source)
XLA Modules:
  0.0 704.6 jit_solution(1375702932699397892)
XLA Ops:
  13.6 22.5 %collective-permute-done = f32[512,2,512]{2,1,0:T(2,128)} collective-permute-done((f32[512,2,512]{2,1,0:T(2,128)}, f32[512,2,512]{2,1,0:T(2,128)}, u32[]{:S(2)}, u32[]{:S(2)}) %collective-permute-start) | collective-permute-done | bytes 2097184 | tf_op jit(solution)/shard_map/ppermute | solution.py:14
  36.2 5.3 pad_maximum_fusion
  43.4 17.1 %while.35 = (s32[]{:T(128)}, f32[1024,2,512]{2,1,0:T(2,128)}, s32[4,3]{1,0:T(4,128)S(1)}, f32[4,256,2,256]{3,2,1,0:T(2,128)}, s32[]{:T(128)}) while((s32[]{:T(128)}, f32[1024,2,512]{2,1,0:T(2,128)}, s32[4,3]{1,0:T(4,128)S(1)}, f32[4,256,2,256]{3,2,1,0:T(2,128)}, s32[]{:T(128)}) %tuple.99), condition=%wide.while_cond, body=%wide.while_body.sunk | while | flops 2 | bytes 1050217 | solution.py:57
  43.9 3.7 bitcast_dynamic-update-slice_fusion.2
  48.2 3.7 bitcast_dynamic-update-slice_fusion.2
  52.5 3.7 bitcast_dynamic-update-slice_fusion.2
  56.8 3.7 bitcast_dynamic-update-slice_fusion.2
  62.3 249.9 %while.36 = (s32[]{:T(128)}, f32[4,256,2,256]{3,2,1,0:T(2,128)}, f32[4,2,256,256]{3,2,0,1:T(8,128)}, f32[256,256]{1,0:T(8,128)}, f32[4,256,2,256]{3,2,1,0:T(2,12...) while((s32[]{:T(128)}, f32[4,256,2,256]{3,2,1,0:T(2,128)}, ...), condition=%wide.region_4.5_spmd.clone.clone, body=%wide.region_0.4_spmd.clone.clone.sunk | while | flops 12915048448 | bytes 82838280 | solution.py:99
  100.1 3.7 fusion.229
  104.4 4.6 fusion.232
  111.7 5.4 add_bitcast_fusion.2
  160.1 3.7 fusion.229
  164.5 4.8 fusion.232
  172.0 5.4 add_bitcast_fusion.2
  177.3 3.9 maximum_add_fusion.2
  212.0 3.7 fusion.231
  222.1 3.7 fusion.229
  226.4 4.5 fusion.232
  233.6 5.4 add_bitcast_fusion.2
  239.0 3.9 maximum_add_fusion.2
  283.7 3.7 fusion.229
  288.1 4.6 fusion.232
  295.3 5.4 add_bitcast_fusion.2
  300.7 3.9 maximum_add_fusion.2
  315.3 207.1 %while.34 = (s32[]{:T(128)}, f32[1024,2,512]{2,1,0:T(2,128)}, s32[4]{0:T(128)S(1)}, s32[4]{0:T(128)S(1)}, f32[4,256,2,256]{3,2,1,0:T(2,128)}, /*index=5*/s32[]{:T(128)}, s32[]{:T(128)}, s32[]{:T(128)}, s32[]{:T(128)}) while((s32[]{:T(128)}, f32[1024,2,512]{2,1,0:T(2,128)}, s32[4]{0:T(128)S(1)}, s32[4]{0:T(128)S(1)}, ...), condition=%wide.region_6.7_spmd, body=%wide.region_5.6_spmd.sunk | while | flops 131080 | bytes 2621641 | solution.py:110
  322.1 44.9 %dynamic_update_slice.21 = f32[1024,2,512]{2,1,0:T(2,128)} dynamic-update-slice(f32[1024,2,512]{2,1,0:T(2,128)} %get-tuple-element.735, f32[256,2,256]{2,1,0:T(2,128)S(1)} %bitcast_add_fusion.2, s32[]{:T(128)S(6)} %select_n.175, s32[]{:T(128)} %constant.116.clone.1..sunk, s32[]{:T(128)S(6)} %select_n.176) | dynamic-update-slice | bytes 1048580 | tf_op jit(solution)/shard_map/while/body/eval_jaxpr/dynamic_update_slice | solution.py:106
  373.8 45.0 %dynamic_update_slice.21 = f32[1024,2,512]{2,1,0:T(2,128)} dynamic-update-slice(f32[1024,2,512]{2,1,0:T(2,128)} %get-tuple-element.735, f32[256,2,256]{2,1,0:T(2,128)S(1)} %bitcast_add_fusion.2, s32[]{:T(128)S(6)} %select_n.175, s32[]{:T(128)} %constant.116.clone.1..sunk, s32[]{:T(128)S(6)} %select_n.176) | dynamic-update-slice | bytes 1048580 | tf_op jit(solution)/shard_map/while/body/eval_jaxpr/dynamic_update_slice | solution.py:106
  425.6 45.0 %dynamic_update_slice.21 = f32[1024,2,512]{2,1,0:T(2,128)} dynamic-update-slice(f32[1024,2,512]{2,1,0:T(2,128)} %get-tuple-element.735, f32[256,2,256]{2,1,0:T(2,128)S(1)} %bitcast_add_fusion.2, s32[]{:T(128)S(6)} %select_n.175, s32[]{:T(128)} %constant.116.clone.1..sunk, s32[]{:T(128)S(6)} %select_n.176) | dynamic-update-slice | bytes 1048580 | tf_op jit(solution)/shard_map/while/body/eval_jaxpr/dynamic_update_slice | solution.py:106
  477.4 45.0 %dynamic_update_slice.21 = f32[1024,2,512]{2,1,0:T(2,128)} dynamic-update-slice(f32[1024,2,512]{2,1,0:T(2,128)} %get-tuple-element.735, f32[256,2,256]{2,1,0:T(2,128)S(1)} %bitcast_add_fusion.2, s32[]{:T(128)S(6)} %select_n.175, s32[]{:T(128)} %constant.116.clone.1..sunk, s32[]{:T(128)S(6)} %select_n.176) | dynamic-update-slice | bytes 1048580 | tf_op jit(solution)/shard_map/while/body/eval_jaxpr/dynamic_update_slice | solution.py:106
  522.3 3.8 slice.43
  532.0 155.4 %all-reduce.3.cloned.1.call-done = (f32[4,2,256,256]{3,2,1,0:T(8,128)}, f32[256,256]{1,0:T(8,128)}) async-done(((f32[4,2,256,256]{3,2,1,0:T(8,128)}, f32[256,256]{1,0:T(8,128)}), (f32[4,2,256,256]{3,2,1,0:T(8,128)}, f32[256,256]{1,0:T(8,128)})) %all-reduce.3.cloned.1.call-update) | async-done | bytes 2359312 | tf_op jit(solution)/shard_map/psum | solution.py:100
  692.7 4.9 divide_subtract_fusion
  (169 shorter events, 210.5 us)
Async XLA Ops:
  7.2 680.3 %all-reduce.3.cloned.1.call-start = ((), (), s32[]{:S(2)}) async-start(), calls=%async_computation | async-start | bytes 4718592 | tf_op jit(solution)/shard_map/psum | solution.py:100
  7.2 29.0 %collective-permute-start = (f32[512,2,512]{2,1,0:T(2,128)}, f32[512,2,512]{2,1,0:T(2,128)}, u32[]{:S(2)}, u32[]{:S(2)}) collective-permute-start(f32[512,2,512]{2,1,0:T(2,128)} %param.9), channel_id=1, source_target_pairs={{8,0},{16,8},{24,16},{32,24},{40,32},{48,40},{56,48},{64,56},{72,6... | collective-permute-start | bytes 6291464 | tf_op jit(solution)/shard_map/ppermute | solution.py:14
  11.7 24.5 %copy-start.7 = (f32[512,2,512]{2,1,0:T(2,128)S(1)}, f32[512,2,512]{2,1,0:T(2,128)}, u32[]{:S(2)}) copy-start(f32[512,2,512]{2,1,0:T(2,128)} %param.9) | copy-start | bytes 6291460
  99.0 1.0 copy-start.1
  104.4 4.6 copy-start.2
  104.4 7.3 %copy-start = (f32[4,256,256]{1,2,0:T(8,128)S(1)}, f32[4,256,256]{1,2,0:T(8,128)}, u32[]{:S(2)}) copy-start(f32[4,256,256]{1,2,0:T(8,128)} %fusion.231) | copy-start | bytes 3145732 | tf_op jit(solution)/shard_map/while
  117.0 3.2 copy-start.5
  159.1 1.0 copy-start.1
  164.5 4.8 copy-start.2
  164.5 7.5 %copy-start = (f32[4,256,256]{1,2,0:T(8,128)S(1)}, f32[4,256,256]{1,2,0:T(8,128)}, u32[]{:S(2)}) copy-start(f32[4,256,256]{1,2,0:T(8,128)} %fusion.231) | copy-start | bytes 3145732 | tf_op jit(solution)/shard_map/while
  177.3 3.9 copy-start.5
  221.0 1.0 copy-start.1
  226.4 4.6 copy-start.2
  226.4 7.2 %copy-start = (f32[4,256,256]{1,2,0:T(8,128)S(1)}, f32[4,256,256]{1,2,0:T(8,128)}, u32[]{:S(2)}) copy-start(f32[4,256,256]{1,2,0:T(8,128)} %fusion.231) | copy-start | bytes 3145732 | tf_op jit(solution)/shard_map/while
  239.0 3.9 copy-start.5
  282.7 1.0 copy-start.1
  288.0 4.6 copy-start.2
  288.1 7.3 %copy-start = (f32[4,256,256]{1,2,0:T(8,128)S(1)}, f32[4,256,256]{1,2,0:T(8,128)}, u32[]{:S(2)}) copy-start(f32[4,256,256]{1,2,0:T(8,128)} %fusion.231) | copy-start | bytes 3145732 | tf_op jit(solution)/shard_map/while
  300.7 3.9 copy-start.5
  522.3 5.7 copy-start.3
  526.1 165.7 %collective-permute-start.1 = (f32[512,2,512]{2,1,0:T(2,128)}, f32[512,2,512]{2,1,0:T(2,128)}, u32[]{:S(2)}, u32[]{:S(2)}) collective-permute-start(f32[512,2,512]{2,1,0:T(2,128)} %slice.43), channel_id=1, source_target_pairs={{0,8},{8,16},{16,24},{24,32},{32,40},{40,48},{48,56},{56,64},{64,7... | collective-permute-start | bytes 6291464 | tf_op jit(solution)/shard_map/ppermute | solution.py:14
  529.6 1.6 copy-start.6
  688.4 3.4 copy-start.4
  688.4 4.2 copy-start.8
Sparse Core Ops, SparseCore 0:
  529.8 157.6 all-reduce.2
where the time goes:
time: 710 us; the launch traced here: 705 us
  local copies, waits for them, and re-layouts  230 us (32%)
  matrix products  201 us (28%)
  waiting for transfers between devices  178 us (25%)
  other arithmetic  53.2 us (7%)
  loops' own time  23.3 us (3%)
  between operations  14.3 us (2%)
    dynamic_update_slice x4, local copies, waits for them, and re-layouts, put(): lax.dynamic_update_slice(scratch_array, current + wgrads[position_entry],...  180 us
    psum x1, waiting for transfers between devices, on_device(): pgrad, cover = lax.psum((pgrad, cover), ('region', 'group'))  155 us
    dot_general x8, matrix products, transform(): jnp.einsum('mjk,kl->mjl', left_i, sin_tab, precision=highest)  32.1 us
    dot_general x8, matrix products, transform(): jnp.einsum('mjk,kl->mjl', left_i, cos_tab, precision=highest)  29.2 us
    dot_general x8, matrix products, transform(): jnp.einsum('jk,mkl->mjl', sin_tab, real_part, precision=highest)  25.5 us
    dot_general x8, matrix products, transform(): jnp.einsum('mjk,kl->mjl', left_r, sin_tab, precision=highest)  25.3 us
    dot_general x8, matrix products, transform(): jnp.einsum('mjk,kl->mjl', left_r, cos_tab, precision=highest)  22.6 us
    ppermute x2, waiting for transfers between devices, shifted(): return lax.ppermute(block, axis, route)  22.5 us
  transfers between devices with their start and end apart: 3, of which 2 were waited for; matrix products, arithmetic and copies ran while one was open for 1% of the time, Pallas kernels for 0%

commit v1 on v0

v1 whole, which is shorter than its diff:
```python
import functools
import math

import jax
import jax.numpy as jnp
import ml_dtypes
import numpy as np
from jax import lax
from jax.experimental import pallas as pl
from jax.experimental.pallas import tpu as pltpu
from jax.sharding import PartitionSpec as P

F32 = jnp.float32
BF16 = jnp.bfloat16
HALF = 128


def split_table(table):
    high = table.astype(np.float32).astype(ml_dtypes.bfloat16)
    low = (table - high.astype(np.float64)).astype(np.float32).astype(ml_dtypes.bfloat16)
    return high, low


def tables():
    n = np.arange(HALF)[:, None].astype(np.float64)
    k = np.arange(HALF)[None, :].astype(np.float64)
    out = {}
    for parity in (0, 1):
        angle = -2.0 * math.pi * ((n * (2 * k + parity)) % 256) / 256
        re, im = np.cos(angle) / 16, np.sin(angle) / 16
        full = np.block([[re, im], [-im, re]])
        high, low = split_table(full)
        out["r", parity] = np.concatenate([high, high, low], axis=0)
        out["rt", parity] = np.concatenate([high.T, high.T, low.T], axis=0)
        out["l", parity] = np.concatenate([high, high, low], axis=1)
        out["lt", parity] = np.concatenate([high.T, high.T, low.T], axis=1)
    perm = np.zeros((256, 256), np.float32)
    for c in range(256):
        perm[c, (c % 2) * HALF + c // 2] = 1
    perm = perm.astype(ml_dtypes.bfloat16)
    return (
        np.stack([out["r", 0], out["r", 1]]),
        np.stack([out["rt", 0], out["rt", 1]]),
        np.stack([out["l", 0], out["l", 1]]),
        np.stack([out["lt", 0], out["lt", 1]]),
        np.concatenate([perm, perm], axis=0),
    )


def parts_of(x):
    high = x.astype(BF16)
    low = (x - high.astype(F32)).astype(BF16)
    return high, low


def mul_right(x, table):
    high, low = parts_of(x)
    return jnp.dot(jnp.concatenate([high, low, high], axis=1), table, preferred_element_type=F32)


def mul_left(table, x):
    high, low = parts_of(x)
    return jnp.dot(table, jnp.concatenate([high, low, high], axis=0), preferred_element_type=F32)


def swap_blocks(a, b):
    return jnp.concatenate(
        [
            jnp.concatenate([a[:, :HALF], b[:, :HALF]], axis=1),
            jnp.concatenate([a[:, HALF:], b[:, HALF:]], axis=1),
        ],
        axis=0,
    )


def compute_kernel(
    rows_ref, cols_ref, count_ref, object_ref, halo_ref, probe_ref, diff_ref,
    r_ref, rt_ref, l_ref, lt_ref, perm_ref,
    part_ref, spill_ref, pgrad_ref, cover_ref,
    ext_ref, acc_ref, win_ref, far_ref, go_ref, factor_ref,
):
    modes = probe_ref.shape[0]
    own = object_ref.shape[0]
    ext_ref[:own] = object_ref[...]
    ext_ref[own:] = halo_ref[...]
    acc_ref[...] = jnp.zeros_like(acc_ref)
    pgrad_ref[...] = jnp.zeros_like(pgrad_ref)
    cover_ref[...] = jnp.zeros_like(cover_ref)

    total = jnp.zeros((256, 256), F32)
    for m in range(modes):
        total = total + probe_ref[m, 0] * probe_ref[m, 0] + probe_ref[m, 1] * probe_ref[m, 1]
    peak = jnp.max(total)

    lane = lax.broadcasted_iota(jnp.int32, (256, HALF), 1)

    def slot_body(s, carry):
        row, col = rows_ref[s], cols_ref[s]
        q, shift = col // HALF, lax.rem(col, HALF)

        def where_at(c, k):
            return pl.ds(row * 8 + jnp.minimum(q + k, 3) * 2 + c, 256, stride=8)

        back = lax.rem(HALF - shift, HALF)
        for c in (0, 1):
            t = [pltpu.roll(ext_ref[where_at(c, k), :], back, axis=1) for k in range(3)]
            for k in (0, 1):
                win_ref[c, :, k * HALF : (k + 1) * HALF] = jnp.where(lane < HALF - shift, t[k], t[k + 1])
        wr, wi = win_ref[0], win_ref[1]
        cover_ref[...] += wr * wr + wi * wi

        def forward(m, carry):
            pr, pi = probe_ref[m, 0], probe_ref[m, 1]
            wr, wi = win_ref[0], win_ref[1]
            er = pr * wr - pi * wi
            ei = pr * wi + pi * wr
            a = jnp.concatenate([er[:, :HALF] + er[:, HALF:], ei[:, :HALF] + ei[:, HALF:]], axis=1)
            b = jnp.concatenate([er[:, :HALF] - er[:, HALF:], ei[:, :HALF] - ei[:, HALF:]], axis=1)
            ye = mul_right(a, r_ref[0])
            yo = mul_right(b, r_ref[1])
            plus = swap_blocks(ye[:HALF] + ye[HALF:], yo[:HALF] + yo[HALF:])
            minus = swap_blocks(ye[:HALF] - ye[HALF:], yo[:HALF] - yo[HALF:])
            far_ref[m, 0] = mul_left(lt_ref[0], plus)
            far_ref[m, 1] = mul_left(lt_ref[1], minus)
            return carry

        lax.fori_loop(0, modes, forward, 0)

        for p in (0, 1):
            intensity = jnp.zeros((HALF, 256), F32)
            for m in range(modes):
                fr, fi = far_ref[m, p, :HALF], far_ref[m, p, HALF:]
                intensity = intensity + (fr * fr + fi * fi)
            wanted = jnp.sqrt(
                jnp.concatenate(
                    [
                        diff_ref[s, h, pl.ds(p, HALF, stride=2), :]
                        for h in (0, 1)
                    ],
                    axis=1,
                )
            )
            high, low = parts_of(wanted)
            wanted = jnp.dot(
                jnp.concatenate([high, low], axis=1), perm_ref[...], preferred_element_type=F32
            )
            factor_ref[p] = 1.0 - wanted / jnp.sqrt(jnp.maximum(intensity, 1.0))

        go_ref[...] = jnp.zeros_like(go_ref)

        def inverse(m, carry):
            ge = far_ref[m, 0] * jnp.concatenate([factor_ref[0], factor_ref[0]], axis=0)
            gd = far_ref[m, 1] * jnp.concatenate([factor_ref[1], factor_ref[1]], axis=0)
            e = mul_left(l_ref[0], ge)
            o = mul_left(l_ref[1], gd)
            top, bottom = e + o, e - o
            ae, ao = [
                jnp.concatenate(
                    [
                        jnp.concatenate([x[:HALF, at : at + HALF], x[HALF:, at : at + HALF]], axis=1)
                        for x in (top, bottom)
                    ],
                    axis=0,
                )
                for at in (0, HALF)
            ]
            e = mul_right(ae, rt_ref[0])
            o = mul_right(ao, rt_ref[1])
            left, right = e + o, e - o
            cr = jnp.concatenate([left[:, :HALF], right[:, :HALF]], axis=1)
            ci = jnp.concatenate([left[:, HALF:], right[:, HALF:]], axis=1)
            pr, pi = probe_ref[m, 0], probe_ref[m, 1]
            wr, wi = win_ref[0], win_ref[1]
            go_ref[0] += pr * cr + pi * ci
            go_ref[1] += pr * ci - pi * cr
            pgrad_ref[m, 0] += wr * cr + wi * ci
            pgrad_ref[m, 1] += wr * ci - wi * cr
            return carry

        lax.fori_loop(0, modes, inverse, 0)

        for c in (0, 1):
            g = [pltpu.roll(go_ref[c, :, k * HALF : (k + 1) * HALF], shift, axis=1) for k in (0, 1)]
            zero = jnp.zeros_like(g[0])
            for k, (here, wrapped) in enumerate(((g[0], zero), (g[1], g[0]), (zero, g[1]))):
                acc_ref[where_at(c, k), :] += jnp.where(lane >= shift, here, wrapped)
        return carry

    lax.fori_loop(0, count_ref[0], slot_body, 0)
    part_ref[...] = object_ref[...] - acc_ref[:own] / peak
    spill_ref[...] = acc_ref[own:] / peak


def compute(rows, cols, count, view, halo, probe, diffraction):
    modes = probe.shape[0]
    slots = diffraction.shape[0]
    consts = [jnp.asarray(t) for t in tables()]
    smem = pl.BlockSpec(memory_space=pltpu.SMEM)
    vmem = pl.BlockSpec(memory_space=pltpu.VMEM)
    diffraction = diffraction.reshape(slots, 256, 2, HALF).transpose(0, 2, 1, 3)
    return pl.pallas_call(
        compute_kernel,
        out_shape=(
            jax.ShapeDtypeStruct(view.shape, F32),
            jax.ShapeDtypeStruct(halo.shape, F32),
            jax.ShapeDtypeStruct(probe.shape, F32),
            jax.ShapeDtypeStruct((256, 256), F32),
        ),
        in_specs=[smem] * 3 + [vmem] * (4 + len(consts)),
        out_specs=[vmem] * 4,
        scratch_shapes=[
            pltpu.VMEM((view.shape[0] + halo.shape[0], HALF), F32),
            pltpu.VMEM((view.shape[0] + halo.shape[0], HALF), F32),
            pltpu.VMEM((2, 256, 256), F32),
            pltpu.VMEM((modes, 2, 256, 256), F32),
            pltpu.VMEM((2, 256, 256), F32),
            pltpu.VMEM((2, HALF, 256), F32),
        ],
        compiler_params=pltpu.CompilerParams(vmem_limit_bytes=48 << 20),
        name="slots",
    )(rows, cols, count, view, halo, probe, diffraction, *consts)


def shifted(block, axis, distance):
    devices = range(lax.axis_size(axis))
    route = [(i - distance, i) for i in devices if i - distance in devices]
    return lax.ppermute(block, axis, route)


def on_device(object_slab, probe, diffraction, positions, slot_counts):
    tile_rows, _, tile_cols = object_slab.shape
    side = probe.shape[2]
    blocks = tile_cols // HALF
    view = (
        object_slab.reshape(tile_rows, 2, blocks, HALF)
        .transpose(0, 2, 1, 3)
        .reshape(tile_rows * blocks * 2, HALF)
    )
    edge = side * blocks * 2
    rows = positions[:, 0] - lax.axis_index("region") * tile_rows
    cols = positions[:, 1]
    halo = shifted(view[:edge], "region", -1)
    part, spill, pgrad, cover = compute(rows, cols, slot_counts[0], view, halo, probe, diffraction)
    pgrad, cover = lax.psum((pgrad, cover), ("region", "group"))
    arrived = shifted(spill, "region", 1)
    part = jnp.concatenate([part[:edge] - arrived, part[edge:]], axis=0)
    obj = (
        part.reshape(tile_rows, blocks, 2, HALF)
        .transpose(0, 2, 1, 3)
        .reshape(tile_rows, 2, tile_cols)
    )
    prb = probe - pgrad / (cover + 1e-06)[None, None]
    return (obj, prb)


def solution(mesh):
    placed = (
        P("region", None, "group"),
        P(),
        P(("region", "group"), None, None),
        P(("region", "group"), None),
        P("group", "region"),
    )
    return jax.shard_map(
        on_device,
        mesh=mesh,
        in_specs=placed,
        out_specs=(P("region", None, "group"), P()),
        check_vma=False,
    )
```

time: 710 us -> 234 us (0.33)
  local copies, waits for them, and re-layouts: 230 us -> 10.6 us
  matrix products: 201 us -> 0 us
  other arithmetic: 53.2 us -> 7.06 us
  loops' own time: 23.3 us -> 0 us
  starting transfers between devices: 5.28 us -> 27.3 us
  waiting for transfers between devices: 178 us -> 160 us
  Pallas kernels: 0 us -> 13.1 us
    dot_general x64 -> x0, matrix products: 201 us -> none  [the longest x8 32.1 us: transform(): jnp.einsum('mjk,kl->mjl', left_i, sin_tab, precision=highest)]
    dynamic_update_slice x4 -> x0, local copies, waits for them, and re-layouts: 180 us -> none  [put(): lax.dynamic_update_slice(scratch_array, current + wgrads[position_entry],...]
    add x13 -> x1, other arithmetic: 29.2 us -> 0.97 us  [on_device(): prb = probe - pgrad / (cover + 1e-06)[None, None]]
    another operation x3 -> x0, loops' own time: 23.3 us -> none  [the longest x1 14.6 us: on_device(): lax.fori_loop(0, slots, put, jnp.zeros(extended.shape, jnp.float32))]
    ppermute x2, starting transfers between devices: 5.24 us -> 27.2 us  [shifted(): return lax.ppermute(block, axis, route)]
    gather x12 -> x0, local copies, waits for them, and re-layouts: 17.1 us -> none
    psum x1, waiting for transfers between devices: 155 us -> 140 us  [on_device(): pgrad, cover = lax.psum((pgrad, cover), ('region', 'group'))]
    pallas_call x0 -> x1, Pallas kernels: none -> 13.1 us  [compute(): pl.pallas_call(compute_kernel, out_shape=(jax.ShapeDtypeStruct(view.shape...]
  transfers between devices with their start and end apart: 3 -> 3, of which waited for: 2 -> 3; matrix products, arithmetic and copies ran while one was open for 1% -> 3% of each run, Pallas kernels for 0% -> 0%
where the time goes in v1:
time: 234 us; the launch traced here: 233 us
  waiting for transfers between devices  160 us (68%)
  starting transfers between devices  27.3 us (12%)
  between operations  14.8 us (6%)
  Pallas kernels  13.1 us (6%)
  local copies, waits for them, and re-layouts  10.6 us (5%)
  other arithmetic  7.06 us (3%)
    psum x1, waiting for transfers between devices, on_device(): pgrad, cover = lax.psum((pgrad, cover), ('region', 'group'))  140 us
    ppermute x2, starting transfers between devices, shifted(): return lax.ppermute(block, axis, route)  27.2 us
    ppermute x2, waiting for transfers between devices, shifted(): return lax.ppermute(block, axis, route)  20.7 us
    pallas_call x1, Pallas kernels, compute(): pl.pallas_call(compute_kernel, out_shape=(jax.ShapeDtypeStruct(view.shape...  13.1 us
    unnamed x19, local copies, waits for them, and re-layouts  5.52 us
  transfers between devices with their start and end apart: 3, of which 3 were waited for; matrix products, arithmetic and copies ran while one was open for 3% of the time, Pallas kernels for 0%

profile of v1, /device:TPU:1, one launch (start us, length us, event | category | flops | bytes accessed | tf_op | source)
XLA Modules:
  0.0 233.2 jit_solution(7588149157029876008)
XLA Ops:
  7.2 0.0 all-reduce.3.cloned.1.call-start
  7.2 2.6 %slice.24 = f32[256,4,2,128]{3,2,1,0:T(2,128)} slice(f32[512,4,2,128]{3,2,1,0:T(2,128)} %bitcast.19), slice={[0:256], [0:4], [0:2], [0:128]} | slice | bytes 2097152 | tf_op jit(solution)/shard_map/slice | solution.py:242
  9.8 3.3 %collective-permute-start = (f32[2048,128]{1,0:T(8,128)}, f32[2048,128]{1,0:T(8,128)S(1)}, u32[]{:S(2)}, u32[]{:S(2)}) collective-permute-start(f32[2048,128]{1,0:T(8,128)} %bitcast.7), channel_id=1, source_target_pairs={{8,0},{16,8},{24,16},{32,24},{40,32},{48,40},{56,48},{64,56},{72,6... | collective-permute-start | bytes 3145736 | tf_op jit(solution)/shard_map/ppermute | solution.py:227
  13.7 0.0 copy-start.8
  13.8 0.0 copy-start
  13.8 0.0 copy-start.1
  13.8 0.0 copy-start.2
  13.8 2.7 %copy.15 = f32[4,256,256]{1,2,0:T(8,128)} copy(f32[4,256,256]{2,1,0:T(8,128)} %param.12) | data formatting | bytes 2097152 | tf_op args[2]
  16.5 2.5 %copy.16 = f32[4,256,2,128]{3,1,2,0:T(8,128)} copy(f32[4,256,2,128]{1,3,2,0:T(8,128)} %bitcast.22) | data formatting | bytes 2097152 | tf_op jit(solution)/shard_map/reshape | solution.py:200
  19.0 0.0 copy-done.8
  19.0 8.4 %collective-permute-done.halo_ref = f32[2048,128]{1,0:T(8,128)S(1)} collective-permute-done((f32[2048,128]{1,0:T(8,128)}, f32[2048,128]{1,0:T(8,128)S(1)}, u32[]{:S(2)}, u32[]{:S(2)}) %collective-permute-start) | collective-permute-done | bytes 1048608 | tf_op jit(solution)/shard_map/ppermute | solution.py:227
  27.4 0.0 copy-done
  27.4 0.0 copy-done.1
  27.4 0.0 copy-done.2
  27.4 0.0 copy-start.3
  27.4 1.1 copy-done.3
  28.5 0.0 copy-start.4
  28.5 0.9 copy-done.4
  29.5 13.1 %slots.1 = (f32[4096,128]{1,0:T(8,128)}, f32[2048,128]{1,0:T(8,128)}, f32[4,2,256,256]{3,2,1,0:T(8,128)}, f32[256,256]{1,0:T(8,128)S(1)}) custom-call(s32[4]{0:T(128)S(1)} %get-tuple-element.15.rows_ref, s32[4]{0:T(128)S(1)} %get-tuple-element.14.cols_ref, s32[1]{0:T(128)} %bitcast.18.count_ref, f32[4096,128]{1,0:T(8,128)} %bitcast.20, ...), custom_call_target="tpu_custom_call" | custom-call | tf_op jit(solution)/shard_map/slots/pallas_call | solution.py:201
  42.6 0.0 copy-start.5
  42.6 0.7 copy-done.5
  43.3 23.9 %collective-permute-start.1 = (f32[2048,128]{1,0:T(8,128)}, f32[2048,128]{1,0:T(8,128)}, u32[]{:S(2)}, u32[]{:S(2)}) collective-permute-start(f32[2048,128]{1,0:T(8,128)} %get-tuple-element.7), channel_id=1, source_target_pairs={{0,8},{8,16},{16,24},{24,32},{32,40},{40,48},{48,56},{56,64},{64,7... | collective-permute-start | bytes 3145736 | tf_op jit(solution)/shard_map/ppermute | solution.py:227
  67.3 0.0 all-reduce.3.cloned.1.call-update
  67.3 12.4 %collective-permute-done.1 = f32[2048,128]{1,0:T(8,128)} collective-permute-done((f32[2048,128]{1,0:T(8,128)}, f32[2048,128]{1,0:T(8,128)}, u32[]{:S(2)}, u32[]{:S(2)}) %collective-permute-start.1) | collective-permute-done | bytes 1048608 | tf_op jit(solution)/shard_map/ppermute | solution.py:227
  79.6 0.0 copy-done.7
  79.7 1.4 slice_subtract_fusion
  81.1 0.0 copy-start.6
  81.1 1.5 pad_maximum_fusion
  82.5 139.6 %all-reduce.3.cloned.1.call-done = (f32[4,2,256,256]{3,2,1,0:T(8,128)}, f32[256,256]{1,0:T(8,128)}) async-done(((f32[4,2,256,256]{3,2,1,0:T(8,128)}, f32[256,256]{1,0:T(8,128)}), (f32[4,2,256,256]{3,2,1,0:T(8,128)}, f32[256,256]{1,0:T(8,128)})) %all-reduce.3.cloned.1.call-update) | async-done | bytes 2359312 | tf_op jit(solution)/shard_map/psum | solution.py:244
  222.1 1.0 broadcast_add_fusion
  223.1 0.0 copy-done.6
  223.1 3.2 %divide_subtract_fusion = f32[4,2,256,256]{3,2,1,0:T(8,128)} fusion(f32[4,2,256,256]{3,2,1,0:T(8,128)S(1)} %copy-done.6, f32[4,2,256,256]{3,2,1,0:T(8,128)} %get-tuple-element.10, f32[256,256]{1,0:T(8,128)S(1)} %broadcast_add_fusion), kind=kLoop, calls=%fused_computation.1 | loop fusion | flops 1048576 | bytes 6553600 | tf_op jit(solution)/shard_map/sub | solution.py:252
  (2 shorter events, 0.0 us)
Async XLA Ops:
  7.2 215.0 %all-reduce.3.cloned.1.call-start = ((), (), s32[]{:S(2)}) async-start(), calls=%async_computation | async-start | bytes 4718592 | tf_op jit(solution)/shard_map/psum | solution.py:244
  9.8 17.6 %collective-permute-start = (f32[2048,128]{1,0:T(8,128)}, f32[2048,128]{1,0:T(8,128)S(1)}, u32[]{:S(2)}, u32[]{:S(2)}) collective-permute-start(f32[2048,128]{1,0:T(8,128)} %bitcast.7), channel_id=1, source_target_pairs={{8,0},{16,8},{24,16},{32,24},{40,32},{48,40},{56,48},{64,56},{72,6... | collective-permute-start | bytes 3145736 | tf_op jit(solution)/shard_map/ppermute | solution.py:227
  13.7 5.3 %copy-start.8 = (s32[4,2]{0,1:T(2,128)S(1)}, s32[4,2]{0,1:T(2,128)}, u32[]{:S(2)}) copy-start(s32[4,2]{0,1:T(2,128)} %param.13) | copy-start | bytes 100
  13.8 13.6 %copy-start = (bf16[2,768,256]{2,1,0:T(8,128)(2,1)S(1)}, bf16[2,768,256]{2,1,0:T(8,128)(2,1)}, u32[]{:S(2)}) copy-start(bf16[2,768,256]{2,1,0:T(8,128)(2,1)} %constant.20.clone.r_ref) | copy-start | bytes 2359300
  13.8 13.6 %copy-start.1 = (bf16[2,768,256]{2,1,0:T(8,128)(2,1)S(1)}, bf16[2,768,256]{2,1,0:T(8,128)(2,1)}, u32[]{:S(2)}) copy-start(bf16[2,768,256]{2,1,0:T(8,128)(2,1)} %constant.21.clone.rt_ref) | copy-start | bytes 2359300
  13.8 13.6 %copy-start.2 = (bf16[2,256,768]{2,1,0:T(8,128)(2,1)S(1)}, bf16[2,256,768]{2,1,0:T(8,128)(2,1)}, u32[]{:S(2)}) copy-start(bf16[2,256,768]{2,1,0:T(8,128)(2,1)} %constant.22.clone.l_ref) | copy-start | bytes 2359300
  27.4 1.1 copy-start.3
  28.5 0.9 copy-start.4
  42.6 0.7 copy-start.5
  43.3 36.3 %copy-start.7 = (f32[4096,128]{1,0:T(8,128)S(1)}, f32[4096,128]{1,0:T(8,128)}, u32[]{:S(2)}) copy-start(f32[4096,128]{1,0:T(8,128)} %get-tuple-element.6) | copy-start | bytes 6291460
  43.3 36.3 %collective-permute-start.1 = (f32[2048,128]{1,0:T(8,128)}, f32[2048,128]{1,0:T(8,128)}, u32[]{:S(2)}, u32[]{:S(2)}) collective-permute-start(f32[2048,128]{1,0:T(8,128)} %get-tuple-element.7), channel_id=1, source_target_pairs={{0,8},{8,16},{16,24},{24,32},{32,40},{40,48},{48,56},{56,64},{64,7... | collective-permute-start | bytes 3145736 | tf_op jit(solution)/shard_map/ppermute | solution.py:227
  81.1 142.0 %copy-start.6 = (f32[4,2,256,256]{3,2,1,0:T(8,128)S(1)}, f32[4,2,256,256]{3,2,1,0:T(8,128)}, u32[]{:S(2)}) copy-start(f32[4,2,256,256]{3,2,1,0:T(8,128)} %probe_ref.1) | copy-start | bytes 6291460
Sparse Core Ops, SparseCore 0:
  67.4 154.6 all-reduce.2

commit v2 on v1

--- a/solution.py
+++ b/solution.py
@@ -221,6 +221,195 @@
     )(rows, cols, count, view, halo, probe, diffraction, *consts)
 
 
+MESH = pl.DeviceIdType.MESH
+ORDERS = (("x", "y", "z"), ("y", "z", "x"), ("z", "x", "y"))
+
+
+def place():
+    region, group = lax.axis_index("region"), lax.axis_index("group")
+    core = lax.rem(region, 2)
+    z = lax.rem(region // 2, 4)
+    y = (group // 4) * 2 + region // 8
+    x = lax.rem(group, 4)
+    return {"x": x, "y": y, "z": z}, core
+
+
+def device(at, core):
+    region = (lax.rem(at["y"], 2) * 4 + at["z"]) * 2 + core
+    return (region, (at["y"] // 2) * 4 + at["x"])
+
+
+def index(fixed):
+    return tuple(fixed.get(axis, slice(None)) for axis in ("x", "y", "z"))
+
+
+def reduce_kernel(
+    pgrad_ref, cover_ref, probe_ref, spill_ref,
+    new_ref, arrived_ref,
+    mate_ref, sum_ref, got1, got2, got3, sum1, sum2, send_sem, recv_sem,
+):
+    me, core = place()
+    regions = lax.axis_size("region")
+    region, group = lax.axis_index("region"), lax.axis_index("group")
+    mate = device(me, 1 - core)
+    up = (lax.rem(region + 1, regions), group)
+    down = (lax.rem(region + regions - 1, regions), group)
+
+    def along(axis, distance):
+        return {**me, axis: lax.rem(me[axis] + distance, 4)}
+
+    barrier = pltpu.get_barrier_semaphore()
+    partners = [mate, up, down]
+    partners += [device(along(axis, d), core) for axis in ("x", "y", "z") for d in (1, 2, 3)]
+    for partner in partners:
+        pl.semaphore_signal(barrier, inc=1, device_id=partner, device_id_type=MESH)
+    pl.semaphore_wait(barrier, len(partners))
+
+    started = []
+
+    def send(src, dst, to):
+        n = len(started)
+        copy = pltpu.make_async_remote_copy(
+            src_ref=src, dst_ref=dst, send_sem=send_sem.at[n], recv_sem=recv_sem.at[n],
+            device_id=to, device_id_type=MESH,
+        )
+        copy.start()
+        started.append(copy)
+        return copy
+
+    planes = ((0, 2), (2, 4), (4, 5))
+    mine, theirs = 4 * core, 4 * (1 - core)
+    first = []
+    for p, (lo, hi) in enumerate(planes):
+        src = cover_ref if p == 2 else pgrad_ref.at[pl.ds(theirs + lo, hi - lo)]
+        first.append(send(src, mate_ref.at[lo:hi], mate))
+    spilled = send(spill_ref, arrived_ref, up)
+
+    def exchange(p, axis, source, target):
+        copies = []
+        for d in (1, 2, 3):
+            to = along(axis, d)
+            copies.append(send(source(to[axis]), target.at[d - 1], device(to, core)))
+        return copies
+
+    copies = []
+    for p, (lo, hi) in enumerate(planes):
+        first[p].wait_recv()
+        own = cover_ref[...] if p == 2 else pgrad_ref[pl.ds(mine + lo, hi - lo)]
+        sum_ref[lo:hi] = own + mate_ref[lo:hi]
+        a = ORDERS[p][0]
+        copies.append(
+            exchange(p, a, lambda q: sum_ref.at[(slice(lo, hi), *index({a: q}))], got1.at[:, lo:hi])
+        )
+    later = []
+    for p, (lo, hi) in enumerate(planes):
+        a, b, _ = ORDERS[p]
+        for copy in copies[p]:
+            copy.wait_recv()
+        sum1[lo:hi] = (
+            sum_ref[(slice(lo, hi), *index({a: me[a]}))]
+            + got1[0, lo:hi] + got1[1, lo:hi] + got1[2, lo:hi]
+        )
+        rest = [axis for axis in ("x", "y", "z") if axis != a]
+
+        def part1(q, lo=lo, hi=hi, b=b, rest=rest):
+            return (slice(lo, hi), *(q if axis == b else slice(None) for axis in rest))
+
+        later.append((part1, exchange(p, b, lambda q: sum1.at[part1(q)], got2.at[:, lo:hi])))
+    last = []
+    for p, (lo, hi) in enumerate(planes):
+        _, b, c = ORDERS[p]
+        part1, arriving = later[p]
+        for copy in arriving:
+            copy.wait_recv()
+        sum2[lo:hi] = sum1[part1(me[b])] + got2[0, lo:hi] + got2[1, lo:hi] + got2[2, lo:hi]
+        last.append(exchange(p, c, lambda q: sum2.at[lo:hi, q], got3.at[:, lo:hi]))
+    reduced = {}
+    for p in (2, 0, 1):
+        lo, hi = planes[p]
+        c = ORDERS[p][2]
+        for copy in last[p]:
+            copy.wait_recv()
+        reduced[p] = sum2[lo:hi, me[c]] + got3[0, lo:hi] + got3[1, lo:hi] + got3[2, lo:hi]
+    here = index(me)
+    steps = []
+    for p in (0, 1):
+        at = pl.ds(mine + 2 * p, 2)
+        new_ref[(at, *here)] = probe_ref[(at, *here)] - reduced[p] / (reduced[2] + 1e-06)
+
+    def spread(p, axis, fixed):
+        at = (pl.ds(mine + 2 * p, 2), *index({f: me[f] for f in fixed}))
+        return [
+            send(new_ref.at[at], new_ref.at[at], device(along(axis, d), core)) for d in (1, 2, 3)
+        ]
+
+    copies = [spread(p, ORDERS[p][2], ORDERS[p]) for p in (0, 1)]
+    for level in (1, 0):
+        following = []
+        for p in (0, 1):
+            for copy in copies[p]:
+                copy.wait_recv()
+            following.append(spread(p, ORDERS[p][level], ORDERS[p][: level + 1]))
+        copies = following
+    final = []
+    for p in (0, 1):
+        a = ORDERS[p][0]
+        planes_at = pl.ds(mine + 2 * p, 2)
+        at = (planes_at, *index({a: me[a]}))
+        final.append(send(new_ref.at[at], new_ref.at[at], mate))
+    for d in (1, 2, 3):
+        for p in (0, 1):
+            a = ORDERS[p][0]
+            copies[p][d - 1].wait_recv()
+            at = (pl.ds(mine + 2 * p, 2), *index({a: lax.rem(me[a] + 4 - d, 4)}))
+            final.append(send(new_ref.at[at], new_ref.at[at], mate))
+    for copy in final:
+        copy.wait_recv()
+    spilled.wait_recv()
+    for copy in started:
+        copy.wait_send()
+
+
+def tiled(planes):
+    return (
+        planes.reshape(-1, 32, 8, 2, HALF).transpose(0, 1, 3, 2, 4).reshape(-1, 4, 4, 4, 8, HALF)
+    )
+
+
+def untiled(tiles, shape):
+    return tiles.reshape(-1, 32, 2, 8, HALF).transpose(0, 1, 3, 2, 4).reshape(shape)
+
+
+def reduce(pgrad, cover, probe, spill):
+    vmem = pl.BlockSpec(memory_space=pltpu.VMEM)
+    count = 3 + 1 + 27 + 18 + 8
+    new, arrived = pl.pallas_call(
+        reduce_kernel,
+        out_shape=(
+            jax.ShapeDtypeStruct((8, 4, 4, 4, 8, HALF), F32),
+            jax.ShapeDtypeStruct(spill.shape, F32),
+        ),
+        in_specs=[vmem] * 4,
+        out_specs=[vmem] * 2,
+        scratch_shapes=[
+            pltpu.VMEM((5, 4, 4, 4, 8, HALF), F32),
+            pltpu.VMEM((5, 4, 4, 4, 8, HALF), F32),
+            pltpu.VMEM((3, 5, 4, 4, 8, HALF), F32),
+            pltpu.VMEM((3, 5, 4, 8, HALF), F32),
+            pltpu.VMEM((3, 5, 8, HALF), F32),
+            pltpu.VMEM((5, 4, 4, 8, HALF), F32),
+            pltpu.VMEM((5, 4, 8, HALF), F32),
+            pltpu.SemaphoreType.DMA((count,)),
+            pltpu.SemaphoreType.DMA((count,)),
+        ],
+        compiler_params=pltpu.CompilerParams(
+            vmem_limit_bytes=40 << 20, collective_id=0, has_side_effects=True
+        ),
+        name="reduce",
+    )(tiled(pgrad), tiled(cover), tiled(probe), spill)
+    return untiled(new, probe.shape), arrived
+
+
 def shifted(block, axis, distance):
     devices = range(lax.axis_size(axis))
     route = [(i - distance, i) for i in devices if i - distance in devices]
@@ -241,15 +430,13 @@
     cols = positions[:, 1]
     halo = shifted(view[:edge], "region", -1)
     part, spill, pgrad, cover = compute(rows, cols, slot_counts[0], view, halo, probe, diffraction)
-    pgrad, cover = lax.psum((pgrad, cover), ("region", "group"))
-    arrived = shifted(spill, "region", 1)
+    prb, arrived = reduce(pgrad, cover, probe, spill)
     part = jnp.concatenate([part[:edge] - arrived, part[edge:]], axis=0)
     obj = (
         part.reshape(tile_rows, blocks, 2, HALF)
         .transpose(0, 2, 1, 3)
         .reshape(tile_rows, 2, tile_cols)
     )
-    prb = probe - pgrad / (cover + 1e-06)[None, None]
     return (obj, prb)
 
 

time: 234 us -> 112 us (0.48)
  waiting for transfers between devices: 160 us -> 8.36 us
  Pallas kernels: 13.1 us -> 84.3 us
  starting transfers between devices: 27.3 us -> 3.32 us
  between operations: 14.8 us -> 1.37 us
  other arithmetic: 7.06 us -> 1.63 us
    psum x1 -> x0, waiting for transfers between devices: 140 us -> none  [on_device(): pgrad, cover = lax.psum((pgrad, cover), ('region', 'group'))]
    pallas_call x0 -> x1, Pallas kernels: none -> 64 us  [reduce(): pl.pallas_call(reduce_kernel, out_shape=(jax.ShapeDtypeStruct((8, 4, 4, 4...]
    ppermute x2 -> x1, starting transfers between devices: 27.2 us -> 3.32 us  [shifted(): return lax.ppermute(block, axis, route)]
    ppermute x2 -> x1, waiting for transfers between devices: 20.7 us -> 8.36 us  [shifted(): return lax.ppermute(block, axis, route)]
    pallas_call x1, Pallas kernels: 13.1 us -> 20.3 us  [compute(): pl.pallas_call(compute_kernel, out_shape=(jax.ShapeDtypeStruct(view.shape...]
    sub x1 -> x0, other arithmetic: 3.23 us -> none  [on_device(): prb = probe - pgrad / (cover + 1e-06)[None, None]]
    unnamed x19 -> x20, local copies, waits for them, and re-layouts: 5.52 us -> 7.7 us
  transfers between devices with their start and end apart: 3 -> 1, of which waited for: 3 -> 1; matrix products, arithmetic and copies ran while one was open for 3% -> 5% of each run, Pallas kernels for 0% -> 0%
where the time goes in v2:
time: 112 us
  Pallas kernels  84.3 us (75%)
  local copies, waits for them, and re-layouts  12.8 us (11%)
  waiting for transfers between devices  8.36 us (7%)
  starting transfers between devices  3.32 us (3%)
  other arithmetic  1.63 us (1%)
  between operations  1.37 us (1%)
    pallas_call x1, Pallas kernels, reduce(): pl.pallas_call(reduce_kernel, out_shape=(jax.ShapeDtypeStruct((8, 4, 4, 4...  64 us
    pallas_call x1, Pallas kernels, compute(): pl.pallas_call(compute_kernel, out_shape=(jax.ShapeDtypeStruct(view.shape...  20.3 us
    ppermute x1, waiting for transfers between devices, shifted(): return lax.ppermute(block, axis, route)  8.36 us
    unnamed x20, local copies, waits for them, and re-layouts  7.7 us
    ppermute x1, starting transfers between devices, shifted(): return lax.ppermute(block, axis, route)  3.32 us
    slice x1, local copies, waits for them, and re-layouts, on_device(): halo = shifted(view[:edge], 'region', -1)  2.56 us
    reshape x1, local copies, waits for them, and re-layouts, compute(): diffraction = diffraction.reshape(slots, 256, 2, HALF).transpose(0, 2, 1, 3)  2.53 us
  transfers between devices with their start and end apart: 1, of which 1 were waited for; matrix products, arithmetic and copies ran while one was open for 5% of the time, Pallas kernels for 0%

profile of v2, /device:TPU:1, one launch (start us, length us, event | category | flops | bytes accessed | tf_op | source)
XLA Modules:
  0.0 111.7 jit_solution(16922366425218569061)
XLA Ops:
  0.6 2.6 %slice.24 = f32[256,4,2,128]{3,2,1,0:T(2,128)} slice(f32[512,4,2,128]{3,2,1,0:T(2,128)} %bitcast.43), slice={[0:256], [0:4], [0:2], [0:128]} | slice | bytes 2097152 | tf_op jit(solution)/shard_map/slice | solution.py:431
  3.2 3.3 %collective-permute-start = (f32[2048,128]{1,0:T(8,128)}, f32[2048,128]{1,0:T(8,128)S(1)}, u32[]{:S(2)}, u32[]{:S(2)}) collective-permute-start(f32[2048,128]{1,0:T(8,128)} %bitcast.7), channel_id=1, source_target_pairs={{8,0},{16,8},{24,16},{32,24},{40,32},{48,40},{56,48},{64,56},{72,6... | collective-permute-start | bytes 3145736 | tf_op jit(solution)/shard_map/ppermute | solution.py:416
  7.2 0.0 copy-start.8
  7.2 0.0 copy-start.2
  7.2 0.0 copy-start.3
  7.2 0.0 copy-start.4
  7.2 2.7 %copy.15 = f32[4,256,256]{1,2,0:T(8,128)} copy(f32[4,256,256]{2,1,0:T(8,128)} %param.12) | data formatting | bytes 2097152 | tf_op args[2]
  9.9 2.5 %copy.16 = f32[4,256,2,128]{3,1,2,0:T(8,128)} copy(f32[4,256,2,128]{1,3,2,0:T(8,128)} %bitcast.46) | data formatting | bytes 2097152 | tf_op jit(solution)/shard_map/reshape | solution.py:200
  12.4 0.0 copy-done.8
  12.4 8.4 %collective-permute-done.halo_ref = f32[2048,128]{1,0:T(8,128)S(1)} collective-permute-done((f32[2048,128]{1,0:T(8,128)}, f32[2048,128]{1,0:T(8,128)S(1)}, u32[]{:S(2)}, u32[]{:S(2)}) %collective-permute-start) | collective-permute-done | bytes 1048608 | tf_op jit(solution)/shard_map/ppermute | solution.py:416
  20.8 0.0 copy-done.2
  20.8 0.0 copy-done.3
  20.8 0.0 copy-done.4
  20.8 0.0 copy-start.5
  20.8 1.1 %copy-done.5 = bf16[2,768,256]{2,1,0:T(8,128)(2,1)S(1)} copy-done((bf16[2,768,256]{2,1,0:T(8,128)(2,1)S(1)}, bf16[2,768,256]{2,1,0:T(8,128)(2,1)}, u32[]{:S(2)}) %copy-start.5) | copy-done | bytes 786456
  21.9 0.0 copy-start.6
  21.9 0.9 copy-done.6
  22.9 0.0 copy-start
  22.9 20.3 %slots.1 = (f32[4096,128]{1,0:T(8,128)}, f32[2048,128]{1,0:T(8,128)S(1)}, f32[4,2,256,256]{3,2,1,0:T(8,128)}, f32[256,256]{1,0:T(8,128)S(1)}) custom-call(s32[4]{0:T(128)S(1)} %get-tuple-element.17.rows_ref, s32[4]{0:T(128)S(1)} %get-tuple-element.16.cols_ref, s32[1]{0:T(128)} %bitcast.38.count_ref, f32[4096,128]{1,0:T(8,128)} %bitcast.44, ...), custom_call_target="tpu_custom_call" | custom-call | tf_op jit(solution)/shard_map/slots/pallas_call | solution.py:201
  43.2 0.0 copy-done
  43.2 0.0 copy-start.1
  43.2 1.6 %copy-done.1 = f32[4,2,256,256]{3,2,1,0:T(8,128)S(1)} copy-done((f32[4,2,256,256]{3,2,1,0:T(8,128)S(1)}, f32[4,2,256,256]{3,2,1,0:T(8,128)}, u32[]{:S(2)}) %copy-start.1) | copy-done | bytes 2097176
  44.8 0.0 copy-start.7
  44.8 64.0 %reduce.1 = (f32[8,4,4,4,8,128]{5,4,3,2,1,0:T(8,128)S(1)}, f32[2048,128]{1,0:T(8,128)S(1)}) custom-call(f32[8,4,4,4,8,128]{5,4,3,2,1,0:T(8,128)S(1)} %bitcast.40, f32[1,4,4,4,8,128]{5,4,3,2,1,0:T(8,128)S(1)} %bitcast.42, f32[8,4,4,4,8,128]{5,4,3,2,1,0:T(8,128)S(1)} %bitcast.39, f32[2048,128]{1,0:T(8,128)S(1)} %get-tuple-element.11.spill_ref), custom_call_target="tpu_custom_call" | custom-call | tf_op jit(solution)/shard_map/reduce/pallas_call | solution.py:386
  108.8 0.0 copy-done.7
  108.8 0.2 slice_subtract_fusion
  109.0 1.5 %pad_maximum_fusion = f32[4096,128]{1,0:T(8,128)} fusion(f32[2048,128]{1,0:T(8,128)S(1)} %get-tuple-element.15, f32[2048,128]{1,0:T(8,128)S(1)} %get-tuple-element.14), kind=kLoop, calls=%fused_computation | loop fusion | flops 524288 | bytes 4194304 | tf_op jit(solution)/shard_map/concatenate | solution.py:434
  110.4 1.3 %copy.20 = f32[4,2,256,256]{3,2,1,0:T(8,128)} copy(f32[4,2,256,256]{3,2,1,0:T(8,128)S(1)} %bitcast.41) | data formatting | bytes 4194304
  (1 shorter events, 0.0 us)
Async XLA Ops:
  3.2 17.6 %collective-permute-start = (f32[2048,128]{1,0:T(8,128)}, f32[2048,128]{1,0:T(8,128)S(1)}, u32[]{:S(2)}, u32[]{:S(2)}) collective-permute-start(f32[2048,128]{1,0:T(8,128)} %bitcast.7), channel_id=1, source_target_pairs={{8,0},{16,8},{24,16},{32,24},{40,32},{48,40},{56,48},{64,56},{72,6... | collective-permute-start | bytes 3145736 | tf_op jit(solution)/shard_map/ppermute | solution.py:416
  7.2 5.3 %copy-start.8 = (s32[4,2]{0,1:T(2,128)S(1)}, s32[4,2]{0,1:T(2,128)}, u32[]{:S(2)}) copy-start(s32[4,2]{0,1:T(2,128)} %param.13) | copy-start | bytes 100
  7.2 13.6 %copy-start.2 = (bf16[2,256,768]{2,1,0:T(8,128)(2,1)S(1)}, bf16[2,256,768]{2,1,0:T(8,128)(2,1)}, u32[]{:S(2)}) copy-start(bf16[2,256,768]{2,1,0:T(8,128)(2,1)} %constant.21.clone.lt_ref) | copy-start | bytes 2359300
  7.2 13.6 %copy-start.3 = (bf16[2,256,768]{2,1,0:T(8,128)(2,1)S(1)}, bf16[2,256,768]{2,1,0:T(8,128)(2,1)}, u32[]{:S(2)}) copy-start(bf16[2,256,768]{2,1,0:T(8,128)(2,1)} %constant.20.clone.l_ref) | copy-start | bytes 2359300
  7.2 13.6 %copy-start.4 = (bf16[2,768,256]{2,1,0:T(8,128)(2,1)S(1)}, bf16[2,768,256]{2,1,0:T(8,128)(2,1)}, u32[]{:S(2)}) copy-start(bf16[2,768,256]{2,1,0:T(8,128)(2,1)} %constant.19.clone.rt_ref) | copy-start | bytes 2359300
  20.8 1.1 %copy-start.5 = (bf16[2,768,256]{2,1,0:T(8,128)(2,1)S(1)}, bf16[2,768,256]{2,1,0:T(8,128)(2,1)}, u32[]{:S(2)}) copy-start(bf16[2,768,256]{2,1,0:T(8,128)(2,1)} %constant.18.clone.r_ref) | copy-start | bytes 2359300
  21.9 0.9 copy-start.6
  22.9 20.3 %copy-start = (f32[4,2,256,256]{3,2,1,0:T(8,128)S(1)}, f32[4,2,256,256]{3,2,1,0:T(8,128)}, u32[]{:S(2)}) copy-start(f32[4,2,256,256]{3,2,1,0:T(8,128)} %probe_ref.1) | copy-start | bytes 6291460
  43.2 1.6 %copy-start.1 = (f32[4,2,256,256]{3,2,1,0:T(8,128)S(1)}, f32[4,2,256,256]{3,2,1,0:T(8,128)}, u32[]{:S(2)}) copy-start(f32[4,2,256,256]{3,2,1,0:T(8,128)} %get-tuple-element.9) | copy-start | bytes 6291460
  44.8 64.0 %copy-start.7 = (f32[4096,128]{1,0:T(8,128)S(1)}, f32[4096,128]{1,0:T(8,128)}, u32[]{:S(2)}) copy-start(f32[4096,128]{1,0:T(8,128)} %get-tuple-element.8) | copy-start | bytes 6291460

commit v3 on v1

v3 whole, which is shorter than its diff:
```python
import math

import jax
import jax.numpy as jnp
import ml_dtypes
import numpy as np
from jax import lax
from jax.experimental import pallas as pl
from jax.experimental.pallas import tpu as pltpu
from jax.sharding import PartitionSpec as P

F32 = jnp.float32
BF16 = jnp.bfloat16
HALF = 128
SLOTS = 4
MODES = 4
PAD = 64
MESH = pl.DeviceIdType.MESH
AXES = ("x", "y", "z")
ORDERS = (("x", "y", "z"), ("y", "z", "x"), ("x", "y", "z"), ("y", "z", "x"), ("z", "x", "y"))
DIMS = {"x": (4,), "y": (4,), "z": (2, 2)}


def split_table(table):
    high = table.astype(np.float32).astype(ml_dtypes.bfloat16)
    low = (table - high.astype(np.float64)).astype(np.float32).astype(ml_dtypes.bfloat16)
    return high, low


def tables():
    n = np.arange(HALF)[:, None].astype(np.float64)
    k = np.arange(HALF)[None, :].astype(np.float64)
    direct, turned = [], []
    for parity in (0, 1):
        angle = -2.0 * math.pi * ((n * (2 * k + parity)) % 256) / 256
        re, im = np.cos(angle) / 16, np.sin(angle) / 16
        high, low = split_table(np.block([[re, im], [-im, re]]))
        direct.append(np.stack([high, low]))
        turned.append(np.stack([high.T, low.T]))
    perm = np.zeros((256, 256), np.float32)
    for c in range(256):
        perm[c, (c % 2) * HALF + c // 2] = 1
    return np.stack(direct), np.stack(turned), perm.astype(ml_dtypes.bfloat16)


def parts_of(x):
    high = x.astype(BF16)
    low = (x - high.astype(F32)).astype(BF16)
    return high, low


def mul_right(x, table, p):
    high, low = parts_of(x)
    table = jnp.concatenate([table[p, 0], table[p, 0], table[p, 1]], axis=0)
    return jnp.dot(jnp.concatenate([high, low, high], axis=1), table, preferred_element_type=F32)


def mul_left(table, p, x):
    high, low = parts_of(x)
    table = jnp.concatenate([table[p, 0], table[p, 0], table[p, 1]], axis=1)
    return jnp.dot(table, jnp.concatenate([high, low, high], axis=0), preferred_element_type=F32)


def swap_blocks(a, b):
    return jnp.concatenate(
        [
            jnp.concatenate([a[:, :HALF], b[:, :HALF]], axis=1),
            jnp.concatenate([a[:, HALF:], b[:, HALF:]], axis=1),
        ],
        axis=0,
    )


def place():
    region, group = lax.axis_index("region"), lax.axis_index("group")
    core = lax.rem(region, 2)
    z = lax.rem(region // 2, 4)
    y = (group // 4) * 2 + region // 8
    x = lax.rem(group, 4)
    return {"x": x, "y": y, "z": z}, core


def device(at, core):
    region = (lax.rem(at["y"], 2) * 4 + at["z"]) * 2 + core
    return (region, (at["y"] // 2) * 4 + at["x"])


def dims(axes):
    return sum((DIMS[axis] for axis in AXES if axis in axes), ())


def tile(axes, fixed):
    out = ()
    for axis in AXES:
        if axis in axes and axis in fixed:
            q = fixed[axis]
            out += (q // 2, lax.rem(q, 2)) if axis == "z" else (q,)
        elif axis in axes:
            out += (slice(None),) * len(DIMS[axis])
    return out


def step_kernel(
    pos_ref, count_ref, object_hbm, probe_hbm, diff_hbm, direct_hbm, turned_hbm, perm_hbm,
    out_ref, new_ref,
    ext, win, far, wanted, probe, pgrad, cov, go, hx, strips, direct, turned, perm, diff,
    spill, arrived, mate, total, *rest,
):
    got, part = rest[:15], rest[15:25]
    local_sem, send_sem, recv_sem = rest[25:]
    me, core = place()
    regions = lax.axis_size("region")
    region, group = lax.axis_index("region"), lax.axis_index("group")
    sibling = device(me, 1 - core)
    up = (lax.rem(region + 1, regions), group)
    down = (lax.rem(region + regions - 1, regions), group)
    own = object_hbm.shape[0]
    edge = spill.shape[0]

    loads = [
        pltpu.make_async_copy(src, dst, local_sem.at[n])
        for n, (src, dst) in enumerate(
            [
                (object_hbm, ext.at[:own]),
                (diff_hbm, diff),
                (perm_hbm, perm),
                (probe_hbm, probe),
                (direct_hbm, direct),
                (turned_hbm, turned),
            ]
        )
    ]
    for load in loads:
        load.start()

    def along(axis, distance):
        return {**me, axis: lax.rem(me[axis] + distance, 4)}

    barrier = pltpu.get_barrier_semaphore()
    partners = [sibling, up, down]
    partners += [device(along(axis, d), core) for axis in AXES for d in (1, 2, 3)]
    for partner in partners:
        pl.semaphore_signal(barrier, inc=1, device_id=partner, device_id_type=MESH)
    pl.semaphore_wait(barrier, len(partners))

    builders = {}

    def remote(key, build=None):
        if build is not None:
            builders[key] = (len(builders), build)
        n, build = builders[key]
        src, dst, to = build()
        return pltpu.make_async_remote_copy(
            src_ref=src, dst_ref=dst, send_sem=send_sem.at[n], recv_sem=recv_sem.at[n],
            device_id=to, device_id_type=MESH,
        )

    def send(key, build):
        remote(key, build).start()

    def arrive(key):
        remote(key).wait_recv()

    send("halo", lambda: (object_hbm.at[:edge], ext.at[own:], down))

    def plane_of(u, c):
        return 4 * c + u

    def start_core(u):
        send(
            ("core", u),
            lambda: (cov if u == 4 else pgrad.at[plane_of(u, 1 - core)], mate.at[u], sibling),
        )

    def scatter(u, level, source, lead, axes):
        axis = ORDERS[u][level]

        def build(d):
            to = along(axis, d)
            src = source.at[(*lead, *tile(axes, {axis: to[axis]}))]
            return src, got[3 * u + level].at[d - 1], device(to, core)

        for d in (1, 2, 3):
            send(("rs", u, level, d), lambda d=d: build(d))

    def start_first(u):
        arrive(("core", u))
        total[u] = (cov[...] if u == 4 else pgrad[plane_of(u, core)]) + mate[u]
        scatter(u, 0, total, (u,), AXES)

    def gathered(u, level):
        axis = ORDERS[u][level]
        axes = [f for f in AXES if f not in ORDERS[u][:level]]
        for d in (1, 2, 3):
            arrive(("rs", u, level, d))
        source, lead = (total, (u,)) if level == 0 else (part[2 * u + level - 1], ())
        pieces = got[3 * u + level]
        return source[(*lead, *tile(axes, {axis: me[axis]}))] + pieces[0] + pieces[1] + pieces[2]

    def start_next(u, level):
        part[2 * u + level - 1][...] = gathered(u, level - 1)
        axes = [f for f in AXES if f not in ORDERS[u][:level]]
        scatter(u, level, part[2 * u + level - 1], (), axes)

    def renew(u, coverage):
        at = (plane_of(u, core), *tile(AXES, me))
        new_ref[at] = probe[at] - gathered(u, 2) / (coverage + 1e-06)

    def spread(u, level):
        axis = ORDERS[u][level]
        if level < 2:
            for d in (1, 2, 3):
                arrive(("ag", u, level + 1, d))

        def block():
            known = {f: me[f] for f in ORDERS[u][: level + 1]}
            return new_ref.at[(plane_of(u, core), *tile(AXES, known))]

        for d in (1, 2, 3):
            send(
                ("ag", u, level, d),
                lambda d=d: (block(), block(), device(along(axis, d), core)),
            )
        if level == 0:
            send(("back", u, 0), lambda: (block(), block(), sibling))

    def hand_over(u):
        axis = ORDERS[u][0]

        def block(d):
            known = {axis: lax.rem(me[axis] + 4 - d, 4)}
            return new_ref.at[(plane_of(u, core), *tile(AXES, known))]

        for d in (1, 2, 3):
            arrive(("ag", u, 0, d))
            send(("back", u, d), lambda d=d: (block(d), block(d), sibling))

    def tiles_of(x):
        return x.reshape(4, 4, 2, 8, HALF)

    pgrad[...] = jnp.zeros_like(pgrad)
    cov[...] = jnp.zeros_like(cov)
    go[...] = jnp.zeros_like(go)
    hx[:, :PAD] = jnp.zeros((SLOTS, PAD, 8, HALF), F32)
    hx[:, PAD + 256 :] = jnp.zeros((SLOTS, PAD, 8, HALF), F32)
    loads[1].wait()
    loads[2].wait()

    def prepare(s, carry):
        high, low = parts_of(jnp.sqrt(diff[s]))
        root = jnp.dot(high, perm[...], preferred_element_type=F32) + jnp.dot(
            low, perm[...], preferred_element_type=F32
        )
        for h in (0, 1):
            wanted[s, h] = root[:, h * HALF : (h + 1) * HALF]
        return carry

    lax.fori_loop(0, SLOTS, prepare, 0)

    loads[3].wait()

    def probe_at(m, c):
        return jnp.concatenate(
            [probe[2 * m + c, :, :, :, h].reshape(256, HALF) for h in (0, 1)], axis=1
        )

    power = jnp.zeros((256, 256), F32)
    for m in range(MODES):
        pr, pi = probe_at(m, 0), probe_at(m, 1)
        power = power + pr * pr + pi * pi
    peak = jnp.max(power)
    for load in (loads[0], loads[4], loads[5]):
        load.wait()
    arrive("halo")

    base = region * own

    def spot(s):
        return jnp.clip(pos_ref[s, 0] - base, 0, own - 1), pos_ref[s, 1]

    def pick_columns(col, shape, wide):
        at = lax.broadcasted_iota(jnp.int32, shape, wide)
        narrow = lax.broadcasted_iota(jnp.int32, shape, 1 - wide)
        return jnp.where(at - narrow == col, 1.0, 0.0).astype(BF16)

    def live(s, shape):
        return jnp.where(jnp.full(shape, s, jnp.int32) < count_ref[0, 0], 1.0, 0.0).astype(F32)

    def cut(s, carry):
        row, col = spot(s)
        strips[...] = ext[pl.ds(row, 256)].reshape(256 * 8, HALF)
        pick = pick_columns(col, (512, 256), 0)
        for c in (0, 1):
            strip = jnp.concatenate(
                [strips[pl.ds(2 * k + c, 256, stride=8), :] for k in range(4)], axis=1
            )
            high, low = parts_of(strip)
            win[s, c] = jnp.dot(high, pick, preferred_element_type=F32) + jnp.dot(
                low, pick, preferred_element_type=F32
            )
        wr, wi = win[s, 0], win[s, 1]
        power = live(s, (256, 256)) * (wr * wr + wi * wi)
        for h in (0, 1):
            cov[:, :, :, h] += tiles_of(power[:, h * HALF : (h + 1) * HALF])
        return carry

    lax.fori_loop(0, SLOTS, cut, 0)
    start_core(4)

    def forward(s, carry):
        @pl.when(s == 1)
        def _():
            start_first(4)

        @pl.when(s == 2)
        def _():
            start_next(4, 1)

        @pl.when(s == 3)
        def _():
            start_next(4, 2)

        wr, wi = win[s, 0], win[s, 1]
        for m in range(MODES):
            pr, pi = probe_at(m, 0), probe_at(m, 1)
            er = pr * wr - pi * wi
            ei = pr * wi + pi * wr
            a = jnp.concatenate([er[:, :HALF] + er[:, HALF:], ei[:, :HALF] + ei[:, HALF:]], axis=1)
            b = jnp.concatenate([er[:, :HALF] - er[:, HALF:], ei[:, :HALF] - ei[:, HALF:]], axis=1)
            ye = mul_right(a, direct, 0)
            yo = mul_right(b, direct, 1)
            plus = swap_blocks(ye[:HALF] + ye[HALF:], yo[:HALF] + yo[HALF:])
            minus = swap_blocks(ye[:HALF] - ye[HALF:], yo[:HALF] - yo[HALF:])
            far[s, m, 0] = mul_left(turned, 0, plus)
            far[s, m, 1] = mul_left(turned, 1, minus)
        for p in (0, 1):
            intensity = jnp.zeros((HALF, 256), F32)
            for m in range(MODES):
                fr, fi = far[s, m, p, :HALF], far[s, m, p, HALF:]
                intensity = intensity + (fr * fr + fi * fi)
            root = jnp.concatenate(
                [wanted[s, h, pl.ds(p, HALF, stride=2), :] for h in (0, 1)], axis=1
            )
            factor = live(s, (HALF, 256)) * (1.0 - root / jnp.sqrt(jnp.maximum(intensity, 1.0)))
            for m in range(MODES):
                far[s, m, p, :HALF] = far[s, m, p, :HALF] * factor
                far[s, m, p, HALF:] = far[s, m, p, HALF:] * factor
        return carry

    lax.fori_loop(0, SLOTS, forward, 0)

    def inverse(s, pair):
        wr, wi = win[s, 0], win[s, 1]
        for m in pair:
            e = mul_left(direct, 0, far[s, m, 0])
            o = mul_left(direct, 1, far[s, m, 1])
            top, bottom = e + o, e - o
            ae, ao = [
                jnp.concatenate(
                    [
                        jnp.concatenate([x[:HALF, at : at + HALF], x[HALF:, at : at + HALF]], axis=1)
                        for x in (top, bottom)
                    ],
                    axis=0,
                )
                for at in (0, HALF)
            ]
            e = mul_right(ae, turned, 0)
            o = mul_right(ao, turned, 1)
            left, right = e + o, e - o
            cr = jnp.concatenate([left[:, :HALF], right[:, :HALF]], axis=1)
            ci = jnp.concatenate([left[:, HALF:], right[:, HALF:]], axis=1)
            pr, pi = probe_at(m, 0), probe_at(m, 1)
            go[s, 0] += pr * cr + pi * ci
            go[s, 1] += pr * ci - pi * cr
            for c, g in enumerate((wr * cr + wi * ci, wr * ci - wi * cr)):
                for h in (0, 1):
                    pgrad[2 * m + c, :, :, :, h] += tiles_of(g[:, h * HALF : (h + 1) * HALF])

    def first_pair(s, carry):
        inverse(s, (0, 2))
        return carry

    lax.fori_loop(0, SLOTS, first_pair, 0)
    start_core(0)
    start_core(1)
    coverage = gathered(4, 2)

    def second_pair(s, carry):
        @pl.when(s == 1)
        def _():
            start_first(0)
            start_first(1)

        @pl.when(s == 2)
        def _():
            start_next(0, 1)
            start_next(1, 1)

        @pl.when(s == 3)
        def _():
            start_next(0, 2)
            start_next(1, 2)

        inverse(s, (1, 3))
        return carry

    lax.fori_loop(0, SLOTS, second_pair, 0)
    start_core(2)
    start_core(3)
    for u in (0, 1):
        renew(u, coverage)
        spread(u, 2)

    def turn(s, carry):
        pick = pick_columns(spot(s)[1], (256, 512), 1)
        for c in (0, 1):
            high, low = parts_of(go[s, c])
            strip = jnp.dot(high, pick, preferred_element_type=F32) + jnp.dot(
                low, pick, preferred_element_type=F32
            )
            for k in range(4):
                strips[pl.ds(2 * k + c, 256, stride=8), :] = strip[:, k * HALF : (k + 1) * HALF]
        hx[s, PAD : PAD + 256] = strips[...].reshape(256, 8, HALF)
        return carry

    lax.fori_loop(0, SLOTS, turn, 0)

    def added(block):
        out = None
        for s in range(SLOTS):
            start = jnp.clip(block * PAD - spot(s)[0] + PAD, 0, PAD + 256)
            piece = hx[s, pl.ds(start, PAD)]
            out = piece if out is None else out + piece
        return out / peak

    blocks = own // PAD

    def below(i, carry):
        spill[pl.ds(i * PAD, PAD)] = added(blocks + i)
        return carry

    lax.fori_loop(0, edge // PAD, below, 0)
    send("spill", lambda: (spill, arrived, up))
    start_first(2)
    start_first(3)

    def within(i, carry):
        at = pl.ds(i * PAD, PAD)
        out_ref[at] = ext[at] - added(i)
        return carry

    lax.fori_loop(0, blocks, within, 0)
    for u in (0, 1):
        spread(u, 1)
    for u in (2, 3):
        start_next(u, 1)
    for u in (0, 1):
        spread(u, 0)
    for u in (2, 3):
        start_next(u, 2)
    for u in (2, 3):
        renew(u, coverage)
        spread(u, 2)
    for u in (0, 1):
        hand_over(u)
    for u in (2, 3):
        spread(u, 1)
    arrive("spill")

    def rest_of(i, carry):
        at = pl.ds(i * PAD, PAD)
        out_ref[at] = out_ref[at] - arrived[at]
        return carry

    lax.fori_loop(0, edge // PAD, rest_of, 0)
    for u in (2, 3):
        spread(u, 0)
    for u in (2, 3):
        hand_over(u)
    for u in range(4):
        for d in range(4):
            arrive(("back", u, d))
    for key in builders:
        remote(key).wait_send()


def tiled(planes):
    return (
        planes.reshape(-1, 32, 8, 2, HALF)
        .transpose(0, 1, 3, 2, 4)
        .reshape(-1, *dims(AXES), 8, HALF)
    )


def untiled(tiles, shape):
    return tiles.reshape(-1, 32, 2, 8, HALF).transpose(0, 1, 3, 2, 4).reshape(shape)


def step(positions, slot_counts, view, probe, diffraction):
    smem = pl.BlockSpec(memory_space=pltpu.SMEM)
    anywhere = pl.BlockSpec(memory_space=pl.ANY)
    vmem = pl.BlockSpec(memory_space=pltpu.VMEM)
    direct, turned, perm = (jnp.asarray(t) for t in tables())
    own = view.shape[0]
    edge = own // 2
    planes = dims(AXES) + (8, HALF)
    got, part = [], []
    for order in ORDERS:
        for level in range(3):
            left = dims([a for a in AXES if a not in order[: level + 1]]) + (8, HALF)
            got.append(pltpu.VMEM((3, *left), F32))
            if level < 2:
                part.append(pltpu.VMEM(left, F32))
    copies = 2 + 5 + 45 + 36 + 16
    return pl.pallas_call(
        step_kernel,
        out_shape=(
            jax.ShapeDtypeStruct(view.shape, F32),
            jax.ShapeDtypeStruct((8, *planes), F32),
        ),
        in_specs=[smem] * 2 + [anywhere] * 6,
        out_specs=[vmem] * 2,
        scratch_shapes=[
            pltpu.VMEM((own + edge, 8, HALF), F32),
            pltpu.VMEM((SLOTS, 2, 256, 256), F32),
            pltpu.VMEM((SLOTS, MODES, 2, 256, 256), F32),
            pltpu.VMEM((SLOTS, 2, 256, HALF), F32),
            pltpu.VMEM((8, *planes), F32),
            pltpu.VMEM((8, *planes), F32),
            pltpu.VMEM(planes, F32),
            pltpu.VMEM((SLOTS, 2, 256, 256), F32),
            pltpu.VMEM((SLOTS, 256 + 2 * PAD, 8, HALF), F32),
            pltpu.VMEM((256 * 8, HALF), F32),
            pltpu.VMEM(direct.shape, BF16),
            pltpu.VMEM(turned.shape, BF16),
            pltpu.VMEM(perm.shape, BF16),
            pltpu.VMEM(diffraction.shape, F32),
            pltpu.VMEM((edge, 8, HALF), F32),
            pltpu.VMEM((edge, 8, HALF), F32),
            pltpu.VMEM((5, *planes), F32),
            pltpu.VMEM((5, *planes), F32),
            *got,
            *part,
            pltpu.SemaphoreType.DMA((6,)),
            pltpu.SemaphoreType.DMA((copies,)),
            pltpu.SemaphoreType.DMA((copies,)),
        ],
        compiler_params=pltpu.CompilerParams(
            vmem_limit_bytes=60 << 20, collective_id=0, has_side_effects=True
        ),
        name="step",
    )(positions, slot_counts, view, tiled(probe), diffraction, direct, turned, perm)


def on_device(object_slab, probe, diffraction, positions, slot_counts):
    tile_rows, _, tile_cols = object_slab.shape
    blocks = tile_cols // HALF
    view = (
        object_slab.reshape(tile_rows, 2, blocks, HALF)
        .transpose(0, 2, 1, 3)
        .reshape(tile_rows, blocks * 2, HALF)
    )
    view, new = step(positions, slot_counts, view, probe, diffraction)
    obj = (
        view.reshape(tile_rows, blocks, 2, HALF)
        .transpose(0, 2, 1, 3)
        .reshape(tile_rows, 2, tile_cols)
    )
    return (obj, untiled(new, probe.shape))


def solution(mesh):
    placed = (
        P("region", None, "group"),
        P(),
        P(("region", "group"), None, None),
        P(("region", "group"), None),
        P("group", "region"),
    )
    return jax.shard_map(
        on_device,
        mesh=mesh,
        in_specs=placed,
        out_specs=(P("region", None, "group"), P()),
        check_vma=False,
    )
```

time: 234 us -> 104 us (0.44)
  waiting for transfers between devices: 160 us -> 0 us
  Pallas kernels: 13.1 us -> 96.2 us
  starting transfers between devices: 27.3 us -> 0 us
  between operations: 14.8 us -> 1.29 us
  other arithmetic: 7.06 us -> 0 us
  local copies, waits for them, and re-layouts: 10.6 us -> 6.44 us
    psum x1 -> x0, waiting for transfers between devices: 140 us -> none  [on_device(): pgrad, cover = lax.psum((pgrad, cover), ('region', 'group'))]
    pallas_call x1, Pallas kernels: 13.1 us -> 96.2 us  [step(): pl.pallas_call(step_kernel, out_shape=(jax.ShapeDtypeStruct(view.shape, F...]
    ppermute x2 -> x0, starting transfers between devices: 27.2 us -> none  [shifted(): return lax.ppermute(block, axis, route)]
    ppermute x2 -> x0, waiting for transfers between devices: 20.7 us -> none  [shifted(): return lax.ppermute(block, axis, route)]
    sub x2 -> x0, other arithmetic: 4.63 us -> none  [the longest x1 3.23 us: on_device(): prb = probe - pgrad / (cover + 1e-06)[None, None]]
    slice x1 -> x0, local copies, waits for them, and re-layouts: 2.56 us -> none  [on_device(): halo = shifted(view[:edge], 'region', -1)]
    reshape x1 -> x0, local copies, waits for them, and re-layouts: 2.53 us -> none  [compute(): diffraction = diffraction.reshape(slots, 256, 2, HALF).transpose(0, 2, 1, 3)]
    unnamed x19 -> x5, local copies, waits for them, and re-layouts: 5.52 us -> 6.44 us
  transfers between devices with their start and end apart: 3 -> 0, of which waited for: 3 -> 0; matrix products, arithmetic and copies ran while one was open for 3% -> 0% of each run, Pallas kernels for 0% -> 0%
where the time goes in v3:
time: 104 us
  Pallas kernels  96.2 us (92%)
  local copies, waits for them, and re-layouts  6.44 us (6%)
  between operations  1.29 us (1%)
    pallas_call x1, Pallas kernels, step(): pl.pallas_call(step_kernel, out_shape=(jax.ShapeDtypeStruct(view.shape, F...  96.2 us
    unnamed x5, local copies, waits for them, and re-layouts  6.44 us

profile of v3, /device:TPU:1, one launch (start us, length us, event | category | flops | bytes accessed | tf_op | source)
XLA Modules:
  0.0 103.9 jit_solution(2583806586837046470)
XLA Ops:
  1.3 1.3 %copy.11.pos_ref = s32[4,2]{1,0:T(4,128)} copy(s32[4,2]{0,1:T(2,128)} %param.11) | data formatting | bytes 64 | tf_op args[3]
  2.6 96.2 %step.1 = (f32[512,8,128]{2,1,0:T(8,128)}, f32[8,4,4,2,2,8,128]{6,5,4,3,2,1,0:T(8,128)}) custom-call(s32[4,2]{1,0:T(4,128)} %copy.11.pos_ref, s32[1,1]{1,0:T(1,128)S(6)} %copy.15.count_ref, f32[512,8,128]{2,1,0:T(8,128)} %bitcast.20, f32[8,4,4,2,2,8,128]{6,5,4,3,2,1,0:T(8,128)} %bitcast.21, f32[4,256,256]{2,1,0:T(8,128)} %diff_hbm.1, ...), custom_call_target="tpu_custom_call" | custom-call | tf_op jit(solution)/shard_map/step/pallas_call | solution.py:516
  98.8 0.0 copy-start
  98.8 3.8 %copy.16 = f32[512,2,512]{2,1,0:T(2,128)} copy(f32[512,2,512]{2,1,0:T(2,128)} %bitcast.23) | data formatting | bytes 4194304
  102.6 0.0 copy-done
  102.6 1.3 %copy.17 = f32[4,2,256,256]{3,2,1,0:T(8,128)} copy(f32[4,2,256,256]{3,2,1,0:T(8,128)S(1)} %bitcast.22) | data formatting | bytes 4194304
Async XLA Ops:
  98.8 3.8 %copy-start = (f32[8,4,4,2,2,8,128]{6,5,4,3,2,1,0:T(8,128)S(1)}, f32[8,4,4,2,2,8,128]{6,5,4,3,2,1,0:T(8,128)}, u32[]{:S(2)}) copy-start(f32[8,4,4,2,2,8,128]{6,5,4,3,2,1,0:T(8,128)} %get-tuple-element.5) | copy-start | bytes 6291460

commit v4 on v3

--- a/solution.py
+++ b/solution.py
@@ -102,9 +102,9 @@
 
 def step_kernel(
     pos_ref, count_ref, object_hbm, probe_hbm, diff_hbm, direct_hbm, turned_hbm, perm_hbm,
-    out_ref, new_ref,
+    out_ref, arrived, new_ref,
     ext, win, far, wanted, probe, pgrad, cov, go, hx, strips, direct, turned, perm, diff,
-    spill, arrived, mate, total, *rest,
+    spill, mate, total, factor, covered, *rest,
 ):
     got, part = rest[:15], rest[15:25]
     local_sem, send_sem, recv_sem = rest[25:]
@@ -130,9 +130,6 @@
             ]
         )
     ]
-    for load in loads:
-        load.start()
-
     def along(axis, distance):
         return {**me, axis: lax.rem(me[axis] + distance, 4)}
 
@@ -141,6 +138,8 @@
     partners += [device(along(axis, d), core) for axis in AXES for d in (1, 2, 3)]
     for partner in partners:
         pl.semaphore_signal(barrier, inc=1, device_id=partner, device_id_type=MESH)
+    for load in loads:
+        load.start()
     pl.semaphore_wait(barrier, len(partners))
 
     builders = {}
@@ -177,6 +176,8 @@
 
         def build(d):
             to = along(axis, d)
+            if level == 2:
+                return source, got[3 * u + 2].at[me[axis]], device(to, core)
             src = source.at[(*lead, *tile(axes, {axis: to[axis]}))]
             return src, got[3 * u + level].at[d - 1], device(to, core)
 
@@ -202,26 +203,36 @@
         axes = [f for f in AXES if f not in ORDERS[u][:level]]
         scatter(u, level, part[2 * u + level - 1], (), axes)
 
-    def renew(u, coverage):
-        at = (plane_of(u, core), *tile(AXES, me))
-        new_ref[at] = probe[at] - gathered(u, 2) / (coverage + 1e-06)
+    def finish(u):
+        axis = ORDERS[u][2]
+        pieces = got[3 * u + 2]
+        pieces[me[axis]] = part[2 * u + 1][...]
+        for d in (1, 2, 3):
+            arrive(("rs", u, 2, d))
+        reduced = (pieces[0] + pieces[1]) + (pieces[2] + pieces[3])
+        at = tile(AXES, {f: me[f] for f in ORDERS[u][:2]})
+        if u == 4:
+            covered[at] = reduced
+        else:
+            here = (plane_of(u, core), *at)
+            new_ref[here] = probe[here] - reduced / (covered[at] + 1e-06)
 
     def spread(u, level):
         axis = ORDERS[u][level]
-        if level < 2:
+        if level < 1:
             for d in (1, 2, 3):
                 arrive(("ag", u, level + 1, d))
 
         def block():
-            known = {f: me[f] for f in ORDERS[u][: level + 1]}
-            return new_ref.at[(plane_of(u, core), *tile(AXES, known))]
+            at = tile(AXES, {f: me[f] for f in ORDERS[u][: level + 1]})
+            return covered.at[at] if u == 4 else new_ref.at[(plane_of(u, core), *at)]
 
         for d in (1, 2, 3):
             send(
                 ("ag", u, level, d),
                 lambda d=d: (block(), block(), device(along(axis, d), core)),
             )
-        if level == 0:
+        if level == 0 and u < 4:
             send(("back", u, 0), lambda: (block(), block(), sibling))
 
     def hand_over(u):
@@ -276,7 +287,7 @@
     base = region * own
 
     def spot(s):
-        return jnp.clip(pos_ref[s, 0] - base, 0, own - 1), pos_ref[s, 1]
+        return jnp.clip(pos_ref[0, s] - base, 0, own - 1), pos_ref[1, s]
 
     def pick_columns(col, shape, wide):
         at = lax.broadcasted_iota(jnp.int32, shape, wide)
@@ -341,10 +352,9 @@
             root = jnp.concatenate(
                 [wanted[s, h, pl.ds(p, HALF, stride=2), :] for h in (0, 1)], axis=1
             )
-            factor = live(s, (HALF, 256)) * (1.0 - root / jnp.sqrt(jnp.maximum(intensity, 1.0)))
-            for m in range(MODES):
-                far[s, m, p, :HALF] = far[s, m, p, :HALF] * factor
-                far[s, m, p, HALF:] = far[s, m, p, HALF:] * factor
+            factor[s, p] = live(s, (HALF, 256)) * (
+                1.0 - root / jnp.sqrt(jnp.maximum(intensity, 1.0))
+            )
         return carry
 
     lax.fori_loop(0, SLOTS, forward, 0)
@@ -352,8 +362,14 @@
     def inverse(s, pair):
         wr, wi = win[s, 0], win[s, 1]
         for m in pair:
-            e = mul_left(direct, 0, far[s, m, 0])
-            o = mul_left(direct, 1, far[s, m, 1])
+            e, o = [
+                mul_left(
+                    direct,
+                    p,
+                    far[s, m, p] * jnp.concatenate([factor[s, p], factor[s, p]], axis=0),
+                )
+                for p in (0, 1)
+            ]
             top, bottom = e + o, e - o
             ae, ao = [
                 jnp.concatenate(
@@ -378,39 +394,34 @@
                     pgrad[2 * m + c, :, :, :, h] += tiles_of(g[:, h * HALF : (h + 1) * HALF])
 
     def first_pair(s, carry):
+        @pl.when(s == 0)
+        def _():
+            finish(4)
+            spread(4, 1)
+
+        @pl.when(s == 2)
+        def _():
+            spread(4, 0)
+
         inverse(s, (0, 2))
         return carry
 
     lax.fori_loop(0, SLOTS, first_pair, 0)
     start_core(0)
     start_core(1)
-    coverage = gathered(4, 2)
 
     def second_pair(s, carry):
-        @pl.when(s == 1)
+        @pl.when(s == 3)
         def _():
             start_first(0)
             start_first(1)
 
-        @pl.when(s == 2)
-        def _():
-            start_next(0, 1)
-            start_next(1, 1)
-
-        @pl.when(s == 3)
-        def _():
-            start_next(0, 2)
-            start_next(1, 2)
-
         inverse(s, (1, 3))
         return carry
 
     lax.fori_loop(0, SLOTS, second_pair, 0)
     start_core(2)
     start_core(3)
-    for u in (0, 1):
-        renew(u, coverage)
-        spread(u, 2)
 
     def turn(s, carry):
         pick = pick_columns(spot(s)[1], (256, 512), 1)
@@ -425,6 +436,10 @@
         return carry
 
     lax.fori_loop(0, SLOTS, turn, 0)
+    for u in (2, 3):
+        start_first(u)
+    for u in (0, 1):
+        start_next(u, 1)
 
     def added(block):
         out = None
@@ -442,8 +457,10 @@
 
     lax.fori_loop(0, edge // PAD, below, 0)
     send("spill", lambda: (spill, arrived, up))
-    start_first(2)
-    start_first(3)
+    for u in (0, 1):
+        start_next(u, 2)
+    for u in (2, 3):
+        start_next(u, 1)
 
     def within(i, carry):
         at = pl.ds(i * PAD, PAD)
@@ -451,31 +468,23 @@
         return carry
 
     lax.fori_loop(0, blocks, within, 0)
+    for d in (1, 2, 3):
+        arrive(("ag", 4, 0, d))
     for u in (0, 1):
+        finish(u)
         spread(u, 1)
     for u in (2, 3):
-        start_next(u, 1)
+        start_next(u, 2)
     for u in (0, 1):
         spread(u, 0)
     for u in (2, 3):
-        start_next(u, 2)
-    for u in (2, 3):
-        renew(u, coverage)
-        spread(u, 2)
+        finish(u)
+        spread(u, 1)
     for u in (0, 1):
         hand_over(u)
     for u in (2, 3):
-        spread(u, 1)
+        spread(u, 0)
     arrive("spill")
-
-    def rest_of(i, carry):
-        at = pl.ds(i * PAD, PAD)
-        out_ref[at] = out_ref[at] - arrived[at]
-        return carry
-
-    lax.fori_loop(0, edge // PAD, rest_of, 0)
-    for u in (2, 3):
-        spread(u, 0)
     for u in (2, 3):
         hand_over(u)
     for u in range(4):
@@ -509,18 +518,21 @@
     for order in ORDERS:
         for level in range(3):
             left = dims([a for a in AXES if a not in order[: level + 1]]) + (8, HALF)
-            got.append(pltpu.VMEM((3, *left), F32))
             if level < 2:
+                got.append(pltpu.VMEM((3, *left), F32))
                 part.append(pltpu.VMEM(left, F32))
-    copies = 2 + 5 + 45 + 36 + 16
+            else:
+                got.append(pltpu.VMEM((4, *part[-1].shape), F32))
+    copies = 2 + 5 + 45 + 30 + 16
     return pl.pallas_call(
         step_kernel,
         out_shape=(
             jax.ShapeDtypeStruct(view.shape, F32),
+            jax.ShapeDtypeStruct((edge, 8, HALF), F32),
             jax.ShapeDtypeStruct((8, *planes), F32),
         ),
         in_specs=[smem] * 2 + [anywhere] * 6,
-        out_specs=[vmem] * 2,
+        out_specs=[vmem] * 3,
         scratch_shapes=[
             pltpu.VMEM((own + edge, 8, HALF), F32),
             pltpu.VMEM((SLOTS, 2, 256, 256), F32),
@@ -537,9 +549,10 @@
             pltpu.VMEM(perm.shape, BF16),
             pltpu.VMEM(diffraction.shape, F32),
             pltpu.VMEM((edge, 8, HALF), F32),
-            pltpu.VMEM((edge, 8, HALF), F32),
             pltpu.VMEM((5, *planes), F32),
             pltpu.VMEM((5, *planes), F32),
+            pltpu.VMEM((SLOTS, 2, HALF, 256), F32),
+            pltpu.VMEM(planes, F32),
             *got,
             *part,
             pltpu.SemaphoreType.DMA((6,)),
@@ -547,7 +560,7 @@
             pltpu.SemaphoreType.DMA((copies,)),
         ],
         compiler_params=pltpu.CompilerParams(
-            vmem_limit_bytes=60 << 20, collective_id=0, has_side_effects=True
+            vmem_limit_bytes=46 << 20, collective_id=0, has_side_effects=True
         ),
         name="step",
     )(positions, slot_counts, view, tiled(probe), diffraction, direct, turned, perm)
@@ -561,7 +574,9 @@
         .transpose(0, 2, 1, 3)
         .reshape(tile_rows, blocks * 2, HALF)
     )
-    view, new = step(positions, slot_counts, view, probe, diffraction)
+    view, arrived, new = step(positions.T, slot_counts, view, probe, diffraction)
+    edge = arrived.shape[0]
+    view = jnp.concatenate([view[:edge] - arrived, view[edge:]], axis=0)
     obj = (
         view.reshape(tile_rows, blocks, 2, HALF)
         .transpose(0, 2, 1, 3)

time: 104 us -> 96.8 us (0.931)
  Pallas kernels: 96.2 us -> 87.3 us
  other arithmetic: 0 us -> 1.63 us
    pallas_call x1, Pallas kernels: 96.2 us -> 87.3 us  [step(): pl.pallas_call(step_kernel, out_shape=(jax.ShapeDtypeStruct(view.shape, F...]
    concatenate x0 -> x1, other arithmetic: none -> 1.46 us  [on_device(): view = jnp.concatenate([view[:edge] - arrived, view[edge:]], axis=0)]
    unnamed x5 -> x11, local copies, waits for them, and re-layouts: 6.44 us -> 6.2 us
where the time goes in v4:
time: 96.8 us; the launch traced here: 96.5 us
  Pallas kernels  87.3 us (90%)
  local copies, waits for them, and re-layouts  6.2 us (6%)
  other arithmetic  1.63 us (2%)
  between operations  1.31 us (1%)
    pallas_call x1, Pallas kernels, step(): pl.pallas_call(step_kernel, out_shape=(jax.ShapeDtypeStruct(view.shape, F...  87.3 us
    unnamed x11, local copies, waits for them, and re-layouts  6.2 us

profile of v4, /device:TPU:1, one launch (start us, length us, event | category | flops | bytes accessed | tf_op | source)
XLA Modules:
  0.0 96.5 jit_solution(14598771062278575784)
XLA Ops:
  1.3 0.0 copy-start
  1.3 1.2 %copy-done = f32[4,256,256]{2,1,0:T(8,128)S(1)} copy-done((f32[4,256,256]{2,1,0:T(8,128)S(1)}, f32[4,256,256]{2,1,0:T(8,128)}, u32[]{:S(2)}) %copy-start) | copy-done | bytes 1048600
  2.5 0.0 copy-start.1
  2.5 1.0 %copy-done.1 = bf16[2,2,256,256]{3,2,1,0:T(8,128)(2,1)S(1)} copy-done((bf16[2,2,256,256]{3,2,1,0:T(8,128)(2,1)S(1)}, bf16[2,2,256,256]{3,2,1,0:T(8,128)(2,1)}, u32[]{:S(2)}) %copy-start.1) | copy-done | bytes 524312
  3.5 0.0 copy-start.2
  3.5 1.0 %copy-done.2 = bf16[2,2,256,256]{3,2,1,0:T(8,128)(2,1)S(1)} copy-done((bf16[2,2,256,256]{3,2,1,0:T(8,128)(2,1)S(1)}, bf16[2,2,256,256]{3,2,1,0:T(8,128)(2,1)}, u32[]{:S(2)}) %copy-start.2) | copy-done | bytes 524312
  4.6 0.0 copy-start.3
  4.6 0.9 copy-done.3
  5.5 0.0 copy-start.4
  5.5 0.7 copy-done.4
  6.2 87.3 %step.1 = (f32[512,8,128]{2,1,0:T(8,128)S(1)}, f32[256,8,128]{2,1,0:T(8,128)S(1)}, f32[8,4,4,2,2,8,128]{6,5,4,3,2,1,0:T(8,128)S(1)}) custom-call(s32[2,4]{1,0:T(2,128)S(1)} %bitcast.22, s32[1,1]{1,0:T(1,128)S(6)} %copy.13.count_ref, f32[512,8,128]{2,1,0:T(8,128)} %bitcast.23, f32[8,4,4,2,2,8,128]{6,5,4,3,2,1,0:T(8,128)} %bitcast.24, ...), custom_call_target="tpu_custom_call" | custom-call | tf_op jit(solution)/shard_map/step/pallas_call | solution.py:527
  93.5 0.2 slice_subtract_fusion
  93.7 1.5 %pad_maximum_fusion = f32[512,8,128]{2,1,0:T(8,128)} fusion(f32[256,8,128]{2,1,0:T(8,128)S(1)} %get-tuple-element.9, f32[256,8,128]{2,1,0:T(8,128)S(1)} %get-tuple-element.8), kind=kLoop, calls=%fused_computation | loop fusion | flops 524288 | bytes 4194304 | tf_op jit(solution)/shard_map/concatenate | solution.py:579
  95.2 1.3 %copy.14 = f32[4,2,256,256]{3,2,1,0:T(8,128)} copy(f32[4,2,256,256]{3,2,1,0:T(8,128)S(1)} %bitcast.21) | data formatting | bytes 4194304
Async XLA Ops:
  1.3 1.2 %copy-start = (f32[4,256,256]{2,1,0:T(8,128)S(1)}, f32[4,256,256]{2,1,0:T(8,128)}, u32[]{:S(2)}) copy-start(f32[4,256,256]{2,1,0:T(8,128)} %diff_hbm.1) | copy-start | bytes 3145732
  2.5 1.0 %copy-start.1 = (bf16[2,2,256,256]{3,2,1,0:T(8,128)(2,1)S(1)}, bf16[2,2,256,256]{3,2,1,0:T(8,128)(2,1)}, u32[]{:S(2)}) copy-start(bf16[2,2,256,256]{3,2,1,0:T(8,128)(2,1)} %constant.7.clone.turned_hbm) | copy-start | bytes 1572868
  3.5 1.0 %copy-start.2 = (bf16[2,2,256,256]{3,2,1,0:T(8,128)(2,1)S(1)}, bf16[2,2,256,256]{3,2,1,0:T(8,128)(2,1)}, u32[]{:S(2)}) copy-start(bf16[2,2,256,256]{3,2,1,0:T(8,128)(2,1)} %constant.6.clone.direct_hbm) | copy-start | bytes 1572868
  4.6 0.9 copy-start.3
  5.5 0.7 copy-start.4

commit v5 on v4

--- a/solution.py
+++ b/solution.py
@@ -16,9 +16,9 @@
 MODES = 4
 PAD = 64
 MESH = pl.DeviceIdType.MESH
-AXES = ("x", "y", "z")
-ORDERS = (("x", "y", "z"), ("y", "z", "x"), ("x", "y", "z"), ("y", "z", "x"), ("z", "x", "y"))
-DIMS = {"x": (4,), "y": (4,), "z": (2, 2)}
+PLANE = (4, 4, 2, 2, 8, HALF)
+COVERAGE = MODES
+OTHERS = tuple((i, j) for i in range(4) for j in range(4) if (i, j) != (0, 0))
 
 
 def split_table(table):
@@ -77,27 +77,14 @@
     z = lax.rem(region // 2, 4)
     y = (group // 4) * 2 + region // 8
     x = lax.rem(group, 4)
-    return {"x": x, "y": y, "z": z}, core
-
-
-def device(at, core):
-    region = (lax.rem(at["y"], 2) * 4 + at["z"]) * 2 + core
-    return (region, (at["y"] // 2) * 4 + at["x"])
-
-
-def dims(axes):
-    return sum((DIMS[axis] for axis in AXES if axis in axes), ())
-
-
-def tile(axes, fixed):
-    out = ()
-    for axis in AXES:
-        if axis in axes and axis in fixed:
-            q = fixed[axis]
-            out += (q // 2, lax.rem(q, 2)) if axis == "z" else (q,)
-        elif axis in axes:
-            out += (slice(None),) * len(DIMS[axis])
-    return out
+    turned = ((x, y), (y, z), (z, x))
+    return tuple(a + core * (b - a) for a, b in turned), core
+
+
+def device(at, core, counted):
+    a, b, c = at
+    x, y, z = a + counted * (c - a), b + counted * (a - b), c + counted * (b - c)
+    return ((lax.rem(y, 2) * 4 + z) * 2 + core, (y // 2) * 4 + x)
 
 
 def step_kernel(
@@ -106,12 +93,11 @@
     ext, win, far, wanted, probe, pgrad, cov, go, hx, strips, direct, turned, perm, diff,
     spill, mate, total, factor, covered, *rest,
 ):
-    got, part = rest[:15], rest[15:25]
-    local_sem, send_sem, recv_sem = rest[25:]
+    got, pieces, local_sem, send_sem, recv_sem = rest
     me, core = place()
     regions = lax.axis_size("region")
     region, group = lax.axis_index("region"), lax.axis_index("group")
-    sibling = device(me, 1 - core)
+    sibling = device(me, 1 - core, core)
     up = (lax.rem(region + 1, regions), group)
     down = (lax.rem(region + regions - 1, regions), group)
     own = object_hbm.shape[0]
@@ -130,12 +116,15 @@
             ]
         )
     ]
-    def along(axis, distance):
-        return {**me, axis: lax.rem(me[axis] + distance, 4)}
+    def shift(n, distance):
+        return lax.rem(me[n] + distance, 4)
+
+    plane_peers = [(shift(0, i), shift(1, j)) for i, j in OTHERS]
+    plane_devices = [device((p, q, me[2]), core, core) for p, q in plane_peers]
+    last_devices = [device((me[0], me[1], shift(2, d)), core, core) for d in (1, 2, 3)]
 
     barrier = pltpu.get_barrier_semaphore()
-    partners = [sibling, up, down]
-    partners += [device(along(axis, d), core) for axis in AXES for d in (1, 2, 3)]
+    partners = [sibling, up, down, *plane_devices, *last_devices]
     for partner in partners:
         pl.semaphore_signal(barrier, inc=1, device_id=partner, device_id_type=MESH)
     for load in loads:
@@ -162,89 +151,63 @@
 
     send("halo", lambda: (object_hbm.at[:edge], ext.at[own:], down))
 
-    def plane_of(u, c):
-        return 4 * c + u
+    def result(u):
+        return covered if u == COVERAGE else new_ref.at[2 * u + core]
 
     def start_core(u):
         send(
             ("core", u),
-            lambda: (cov if u == 4 else pgrad.at[plane_of(u, 1 - core)], mate.at[u], sibling),
+            lambda: (cov if u == COVERAGE else pgrad.at[2 * u + 1 - core], mate.at[u], sibling),
         )
 
-    def scatter(u, level, source, lead, axes):
-        axis = ORDERS[u][level]
-
-        def build(d):
-            to = along(axis, d)
-            if level == 2:
-                return source, got[3 * u + 2].at[me[axis]], device(to, core)
-            src = source.at[(*lead, *tile(axes, {axis: to[axis]}))]
-            return src, got[3 * u + level].at[d - 1], device(to, core)
-
-        for d in (1, 2, 3):
-            send(("rs", u, level, d), lambda d=d: build(d))
-
-    def start_first(u):
+    def start_plane(u):
         arrive(("core", u))
-        total[u] = (cov[...] if u == 4 else pgrad[plane_of(u, core)]) + mate[u]
-        scatter(u, 0, total, (u,), AXES)
-
-    def gathered(u, level):
-        axis = ORDERS[u][level]
-        axes = [f for f in AXES if f not in ORDERS[u][:level]]
-        for d in (1, 2, 3):
-            arrive(("rs", u, level, d))
-        source, lead = (total, (u,)) if level == 0 else (part[2 * u + level - 1], ())
-        pieces = got[3 * u + level]
-        return source[(*lead, *tile(axes, {axis: me[axis]}))] + pieces[0] + pieces[1] + pieces[2]
-
-    def start_next(u, level):
-        part[2 * u + level - 1][...] = gathered(u, level - 1)
-        axes = [f for f in AXES if f not in ORDERS[u][:level]]
-        scatter(u, level, part[2 * u + level - 1], (), axes)
+        total[u] = (cov[...] if u == COVERAGE else pgrad[2 * u + core]) + mate[u]
+        for n, (p, q) in enumerate(plane_peers):
+            send(
+                ("plane", u, n),
+                lambda n=n, p=p, q=q: (total.at[u, p, q], got.at[u, n], plane_devices[n]),
+            )
+
+    def start_last(u):
+        for n in range(len(OTHERS)):
+            arrive(("plane", u, n))
+        value = total[u, me[0], me[1]]
+        for n in range(len(OTHERS)):
+            value = value + got[u, n]
+        pieces[u, me[2]] = value
+        for n in range(3):
+            send(
+                ("last", u, n),
+                lambda n=n: (pieces.at[u, me[2]], pieces.at[u, me[2]], last_devices[n]),
+            )
 
     def finish(u):
-        axis = ORDERS[u][2]
-        pieces = got[3 * u + 2]
-        pieces[me[axis]] = part[2 * u + 1][...]
-        for d in (1, 2, 3):
-            arrive(("rs", u, 2, d))
-        reduced = (pieces[0] + pieces[1]) + (pieces[2] + pieces[3])
-        at = tile(AXES, {f: me[f] for f in ORDERS[u][:2]})
-        if u == 4:
-            covered[at] = reduced
+        for n in range(3):
+            arrive(("last", u, n))
+        reduced = (pieces[u, 0] + pieces[u, 1]) + (pieces[u, 2] + pieces[u, 3])
+        if u == COVERAGE:
+            covered[me[0], me[1]] = reduced
         else:
-            here = (plane_of(u, core), *at)
-            new_ref[here] = probe[here] - reduced / (covered[at] + 1e-06)
-
-    def spread(u, level):
-        axis = ORDERS[u][level]
-        if level < 1:
-            for d in (1, 2, 3):
-                arrive(("ag", u, level + 1, d))
-
-        def block():
-            at = tile(AXES, {f: me[f] for f in ORDERS[u][: level + 1]})
-            return covered.at[at] if u == 4 else new_ref.at[(plane_of(u, core), *at)]
-
-        for d in (1, 2, 3):
+            here = (2 * u + core, me[0], me[1])
+            new_ref[here] = probe[here] - reduced / (covered[me[0], me[1]] + 1e-06)
+        for n in range(len(OTHERS)):
             send(
-                ("ag", u, level, d),
-                lambda d=d: (block(), block(), device(along(axis, d), core)),
-            )
-        if level == 0 and u < 4:
-            send(("back", u, 0), lambda: (block(), block(), sibling))
+                ("back", u, n),
+                lambda n=n: (
+                    result(u).at[me[0], me[1]],
+                    result(u).at[me[0], me[1]],
+                    plane_devices[n],
+                ),
+            )
+
+    def collect(u):
+        for n in range(len(OTHERS)):
+            arrive(("back", u, n))
 
     def hand_over(u):
-        axis = ORDERS[u][0]
-
-        def block(d):
-            known = {axis: lax.rem(me[axis] + 4 - d, 4)}
-            return new_ref.at[(plane_of(u, core), *tile(AXES, known))]
-
-        for d in (1, 2, 3):
-            arrive(("ag", u, 0, d))
-            send(("back", u, d), lambda d=d: (block(d), block(d), sibling))
+        collect(u)
+        send(("over", u), lambda: (result(u), result(u), sibling))
 
     def tiles_of(x):
         return x.reshape(4, 4, 2, 8, HALF)
@@ -316,20 +279,16 @@
         return carry
 
     lax.fori_loop(0, SLOTS, cut, 0)
-    start_core(4)
+    start_core(COVERAGE)
 
     def forward(s, carry):
         @pl.when(s == 1)
         def _():
-            start_first(4)
-
-        @pl.when(s == 2)
-        def _():
-            start_next(4, 1)
+            start_plane(COVERAGE)
 
         @pl.when(s == 3)
         def _():
-            start_next(4, 2)
+            start_last(COVERAGE)
 
         wr, wi = win[s, 0], win[s, 1]
         for m in range(MODES):
@@ -359,9 +318,9 @@
 
     lax.fori_loop(0, SLOTS, forward, 0)
 
-    def inverse(s, pair):
-        wr, wi = win[s, 0], win[s, 1]
-        for m in pair:
+    def inverse(m, slots):
+        for s in slots:
+            wr, wi = win[s, 0], win[s, 1]
             e, o = [
                 mul_left(
                     direct,
@@ -393,35 +352,21 @@
                 for h in (0, 1):
                     pgrad[2 * m + c, :, :, :, h] += tiles_of(g[:, h * HALF : (h + 1) * HALF])
 
-    def first_pair(s, carry):
-        @pl.when(s == 0)
-        def _():
-            finish(4)
-            spread(4, 1)
-
-        @pl.when(s == 2)
-        def _():
-            spread(4, 0)
-
-        inverse(s, (0, 2))
-        return carry
-
-    lax.fori_loop(0, SLOTS, first_pair, 0)
-    start_core(0)
-    start_core(1)
-
-    def second_pair(s, carry):
-        @pl.when(s == 3)
-        def _():
-            start_first(0)
-            start_first(1)
-
-        inverse(s, (1, 3))
-        return carry
-
-    lax.fori_loop(0, SLOTS, second_pair, 0)
-    start_core(2)
-    start_core(3)
+    for m in range(MODES):
+
+        def of_mode(i, carry, m=m):
+            @pl.when(i == 1)
+            def _():
+                if m == 0:
+                    finish(COVERAGE)
+                else:
+                    start_plane(m - 1)
+
+            inverse(m, (2 * i, 2 * i + 1))
+            return carry
+
+        lax.fori_loop(0, SLOTS // 2, of_mode, 0)
+        start_core(m)
 
     def turn(s, carry):
         pick = pick_columns(spot(s)[1], (256, 512), 1)
@@ -436,10 +381,8 @@
         return carry
 
     lax.fori_loop(0, SLOTS, turn, 0)
-    for u in (2, 3):
-        start_first(u)
-    for u in (0, 1):
-        start_next(u, 1)
+    start_plane(3)
+    start_last(0)
 
     def added(block):
         out = None
@@ -457,10 +400,7 @@
 
     lax.fori_loop(0, edge // PAD, below, 0)
     send("spill", lambda: (spill, arrived, up))
-    for u in (0, 1):
-        start_next(u, 2)
-    for u in (2, 3):
-        start_next(u, 1)
+    start_last(1)
 
     def within(i, carry):
         at = pl.ds(i * PAD, PAD)
@@ -468,28 +408,17 @@
         return carry
 
     lax.fori_loop(0, blocks, within, 0)
-    for d in (1, 2, 3):
-        arrive(("ag", 4, 0, d))
-    for u in (0, 1):
+    start_last(2)
+    finish(0)
+    start_last(3)
+    for u in (1, 2, 3):
         finish(u)
-        spread(u, 1)
-    for u in (2, 3):
-        start_next(u, 2)
-    for u in (0, 1):
-        spread(u, 0)
-    for u in (2, 3):
-        finish(u)
-        spread(u, 1)
-    for u in (0, 1):
+    for u in range(MODES):
         hand_over(u)
-    for u in (2, 3):
-        spread(u, 0)
+    collect(COVERAGE)
     arrive("spill")
-    for u in (2, 3):
-        hand_over(u)
-    for u in range(4):
-        for d in range(4):
-            arrive(("back", u, d))
+    for u in range(MODES):
+        arrive(("over", u))
     for key in builders:
         remote(key).wait_send()
 
@@ -498,7 +427,7 @@
     return (
         planes.reshape(-1, 32, 8, 2, HALF)
         .transpose(0, 1, 3, 2, 4)
-        .reshape(-1, *dims(AXES), 8, HALF)
+        .reshape(-1, *PLANE)
     )
 
 
@@ -508,39 +437,29 @@
 
 def step(positions, slot_counts, view, probe, diffraction):
     smem = pl.BlockSpec(memory_space=pltpu.SMEM)
-    anywhere = pl.BlockSpec(memory_space=pl.ANY)
+    hbm = pl.BlockSpec(memory_space=pltpu.HBM)
     vmem = pl.BlockSpec(memory_space=pltpu.VMEM)
     direct, turned, perm = (jnp.asarray(t) for t in tables())
     own = view.shape[0]
     edge = own // 2
-    planes = dims(AXES) + (8, HALF)
-    got, part = [], []
-    for order in ORDERS:
-        for level in range(3):
-            left = dims([a for a in AXES if a not in order[: level + 1]]) + (8, HALF)
-            if level < 2:
-                got.append(pltpu.VMEM((3, *left), F32))
-                part.append(pltpu.VMEM(left, F32))
-            else:
-                got.append(pltpu.VMEM((4, *part[-1].shape), F32))
-    copies = 2 + 5 + 45 + 30 + 16
+    copies = 2 + (MODES + 1) * (1 + 15 + 3 + 15) + MODES
     return pl.pallas_call(
         step_kernel,
         out_shape=(
             jax.ShapeDtypeStruct(view.shape, F32),
             jax.ShapeDtypeStruct((edge, 8, HALF), F32),
-            jax.ShapeDtypeStruct((8, *planes), F32),
+            jax.ShapeDtypeStruct((8, *PLANE), F32),
         ),
-        in_specs=[smem] * 2 + [anywhere] * 6,
+        in_specs=[smem] * 2 + [hbm] * 6,
         out_specs=[vmem] * 3,
         scratch_shapes=[
             pltpu.VMEM((own + edge, 8, HALF), F32),
             pltpu.VMEM((SLOTS, 2, 256, 256), F32),
             pltpu.VMEM((SLOTS, MODES, 2, 256, 256), F32),
             pltpu.VMEM((SLOTS, 2, 256, HALF), F32),
-            pltpu.VMEM((8, *planes), F32),
-            pltpu.VMEM((8, *planes), F32),
-            pltpu.VMEM(planes, F32),
+            pltpu.VMEM((8, *PLANE), F32),
+            pltpu.VMEM((8, *PLANE), F32),
+            pltpu.VMEM(PLANE, F32),
             pltpu.VMEM((SLOTS, 2, 256, 256), F32),
             pltpu.VMEM((SLOTS, 256 + 2 * PAD, 8, HALF), F32),
             pltpu.VMEM((256 * 8, HALF), F32),
@@ -549,18 +468,18 @@
             pltpu.VMEM(perm.shape, BF16),
             pltpu.VMEM(diffraction.shape, F32),
             pltpu.VMEM((edge, 8, HALF), F32),
-            pltpu.VMEM((5, *planes), F32),
-            pltpu.VMEM((5, *planes), F32),
+            pltpu.VMEM((5, *PLANE), F32),
+            pltpu.VMEM((5, *PLANE), F32),
             pltpu.VMEM((SLOTS, 2, HALF, 256), F32),
-            pltpu.VMEM(planes, F32),
-            *got,
-            *part,
+            pltpu.VMEM(PLANE, F32),
+            pltpu.VMEM((5, len(OTHERS), *PLANE[2:]), F32),
+            pltpu.VMEM((5, 4, *PLANE[2:]), F32),
             pltpu.SemaphoreType.DMA((6,)),
             pltpu.SemaphoreType.DMA((copies,)),
             pltpu.SemaphoreType.DMA((copies,)),
         ],
         compiler_params=pltpu.CompilerParams(
-            vmem_limit_bytes=46 << 20, collective_id=0, has_side_effects=True
+            vmem_limit_bytes=54 << 20, collective_id=0, has_side_effects=True
         ),
         name="step",
     )(positions, slot_counts, view, tiled(probe), diffraction, direct, turned, perm)

time: 96.8 us -> 94.9 us (0.980)
  local copies, waits for them, and re-layouts: 6.2 us -> 2.2 us
  other arithmetic: 1.63 us -> 3.48 us
    unnamed x11 -> x3, local copies, waits for them, and re-layouts: 6.2 us -> 2.2 us
    sub x1, other arithmetic: 0.17 us -> 2.03 us  [on_device(): view = jnp.concatenate([view[:edge] - arrived, view[edge:]], axis=0)]
where the time goes in v5:
time: 94.9 us; the launch traced here: 94.7 us
  Pallas kernels  87.7 us (92%)
  other arithmetic  3.48 us (4%)
  local copies, waits for them, and re-layouts  2.2 us (2%)
  between operations  1.3 us (1%)
    pallas_call x1, Pallas kernels, step(): pl.pallas_call(step_kernel, out_shape=(jax.ShapeDtypeStruct(view.shape, F...  87.7 us
    unnamed x3, local copies, waits for them, and re-layouts  2.2 us
    sub x1, other arithmetic, on_device(): view = jnp.concatenate([view[:edge] - arrived, view[edge:]], axis=0)  2.03 us

profile of v5, /device:TPU:1, one launch (start us, length us, event | category | flops | bytes accessed | tf_op | source)
XLA Modules:
  0.0 94.7 jit_solution(17532561676049204161)
XLA Ops:
  1.3 87.7 %step.1 = (f32[512,8,128]{2,1,0:T(8,128)}, f32[256,8,128]{2,1,0:T(8,128)}, f32[8,4,4,2,2,8,128]{6,5,4,3,2,1,0:T(8,128)}) custom-call(s32[2,4]{1,0:T(2,128)} %bitcast.25, s32[1,1]{1,0:T(1,128)S(6)} %copy.13.count_ref, f32[512,8,128]{2,1,0:T(8,128)} %bitcast.21, f32[8,4,4,2,2,8,128]{6,5,4,3,2,1,0:T(8,128)} %bitcast.22, f32[4,256,256]{2,1,0:T(8,128)} %diff_hbm.1, ...), custom_call_target="tpu_custom_call" | custom-call | tf_op jit(solution)/shard_map/step/pallas_call | solution.py:446
  89.0 2.0 %slice_subtract_fusion = (f32[256,8,128]{2,1,0:T(8,128)S(1)}, f32[256,8,128]{2,1,0:T(8,128)S(1)}) fusion(f32[256,8,128]{2,1,0:T(8,128)} %get-tuple-element.6, f32[512,8,128]{2,1,0:T(8,128)} %get-tuple-element.5), kind=kLoop, calls=%fused_computation.1 | loop fusion | flops 262144 | bytes 5242880 | tf_op jit(solution)/shard_map/sub | solution.py:498
  91.0 0.0 copy-start
  91.1 1.5 %pad_maximum_fusion = f32[512,8,128]{2,1,0:T(8,128)} fusion(f32[256,8,128]{2,1,0:T(8,128)S(1)} %get-tuple-element.9, f32[256,8,128]{2,1,0:T(8,128)S(1)} %get-tuple-element.8), kind=kLoop, calls=%fused_computation | loop fusion | flops 524288 | bytes 4194304 | tf_op jit(solution)/shard_map/concatenate | solution.py:498
  92.5 0.9 copy-done
  93.4 1.3 %copy.14 = f32[4,2,256,256]{3,2,1,0:T(8,128)} copy(f32[4,2,256,256]{3,2,1,0:T(8,128)S(1)} %bitcast.23) | data formatting | bytes 4194304
Async XLA Ops:
  91.0 2.3 %copy-start = (f32[8,4,4,2,2,8,128]{6,5,4,3,2,1,0:T(8,128)S(1)}, f32[8,4,4,2,2,8,128]{6,5,4,3,2,1,0:T(8,128)}, u32[]{:S(2)}) copy-start(f32[8,4,4,2,2,8,128]{6,5,4,3,2,1,0:T(8,128)} %get-tuple-element.7) | copy-start | bytes 6291460

commit v6 on v5

--- a/solution.py
+++ b/solution.py
@@ -17,7 +17,7 @@
 PAD = 64
 MESH = pl.DeviceIdType.MESH
 PLANE = (4, 4, 2, 2, 8, HALF)
-COVERAGE = MODES
+UNITS = ((0, 3), (3, 4), (4, 5))
 OTHERS = tuple((i, j) for i in range(4) for j in range(4) if (i, j) != (0, 0))
 
 
@@ -89,9 +89,9 @@
 
 def step_kernel(
     pos_ref, count_ref, object_hbm, probe_hbm, diff_hbm, direct_hbm, turned_hbm, perm_hbm,
-    out_ref, arrived, new_ref,
+    out_ref, new_ref,
     ext, win, far, wanted, probe, pgrad, cov, go, hx, strips, direct, turned, perm, diff,
-    spill, mate, total, factor, covered, *rest,
+    spill, arrived, mate, total, factor, covered, *rest,
 ):
     got, pieces, local_sem, send_sem, recv_sem = rest
     me, core = place()
@@ -127,8 +127,6 @@
     partners = [sibling, up, down, *plane_devices, *last_devices]
     for partner in partners:
         pl.semaphore_signal(barrier, inc=1, device_id=partner, device_id_type=MESH)
-    for load in loads:
-        load.start()
     pl.semaphore_wait(barrier, len(partners))
 
     builders = {}
@@ -150,64 +148,72 @@
         remote(key).wait_recv()
 
     send("halo", lambda: (object_hbm.at[:edge], ext.at[own:], down))
-
-    def result(u):
-        return covered if u == COVERAGE else new_ref.at[2 * u + core]
-
-    def start_core(u):
+    for load in loads:
+        load.start()
+
+    def start_core(v):
         send(
-            ("core", u),
-            lambda: (cov if u == COVERAGE else pgrad.at[2 * u + 1 - core], mate.at[u], sibling),
+            ("core", v),
+            lambda: (cov if v == 0 else pgrad.at[2 * v - 1 - core], mate.at[v], sibling),
         )
 
     def start_plane(u):
-        arrive(("core", u))
-        total[u] = (cov[...] if u == COVERAGE else pgrad[2 * u + core]) + mate[u]
+        lo, hi = UNITS[u]
+        for v in range(lo, hi):
+            arrive(("core", v))
+            total[v] = (cov[...] if v == 0 else pgrad[2 * v - 2 + core]) + mate[v]
         for n, (p, q) in enumerate(plane_peers):
             send(
                 ("plane", u, n),
-                lambda n=n, p=p, q=q: (total.at[u, p, q], got.at[u, n], plane_devices[n]),
+                lambda n=n, p=p, q=q: (
+                    total.at[lo:hi, p, q],
+                    got.at[n, lo:hi],
+                    plane_devices[n],
+                ),
             )
 
     def start_last(u):
+        lo, hi = UNITS[u]
         for n in range(len(OTHERS)):
             arrive(("plane", u, n))
-        value = total[u, me[0], me[1]]
+        value = total[lo:hi, me[0], me[1]]
         for n in range(len(OTHERS)):
-            value = value + got[u, n]
-        pieces[u, me[2]] = value
+            value = value + got[n, lo:hi]
+        pieces[me[2], lo:hi] = value
         for n in range(3):
             send(
                 ("last", u, n),
-                lambda n=n: (pieces.at[u, me[2]], pieces.at[u, me[2]], last_devices[n]),
+                lambda n=n: (
+                    pieces.at[me[2], lo:hi],
+                    pieces.at[me[2], lo:hi],
+                    last_devices[n],
+                ),
             )
 
     def finish(u):
+        lo, hi = UNITS[u]
         for n in range(3):
             arrive(("last", u, n))
-        reduced = (pieces[u, 0] + pieces[u, 1]) + (pieces[u, 2] + pieces[u, 3])
-        if u == COVERAGE:
-            covered[me[0], me[1]] = reduced
-        else:
-            here = (2 * u + core, me[0], me[1])
-            new_ref[here] = probe[here] - reduced / (covered[me[0], me[1]] + 1e-06)
+        for v in range(lo, hi):
+            reduced = (pieces[0, v] + pieces[1, v]) + (pieces[2, v] + pieces[3, v])
+            if v == 0:
+                covered[...] = reduced + 1e-06
+            else:
+                old = probe[2 * v - 2 + core, me[0], me[1]]
+                new_ref[v - 1, core, me[0], me[1]] = old - reduced / covered[...]
+        here = (slice(max(lo, 1) - 1, hi - 1), core, me[0], me[1])
         for n in range(len(OTHERS)):
             send(
                 ("back", u, n),
-                lambda n=n: (
-                    result(u).at[me[0], me[1]],
-                    result(u).at[me[0], me[1]],
-                    plane_devices[n],
-                ),
-            )
-
-    def collect(u):
+                lambda n=n: (new_ref.at[here], new_ref.at[here], plane_devices[n]),
+            )
+
+    def hand_over(u):
+        lo, hi = UNITS[u]
         for n in range(len(OTHERS)):
             arrive(("back", u, n))
-
-    def hand_over(u):
-        collect(u)
-        send(("over", u), lambda: (result(u), result(u), sibling))
+        whole = (slice(max(lo, 1) - 1, hi - 1), core)
+        send(("over", u), lambda: (new_ref.at[whole], new_ref.at[whole], sibling))
 
     def tiles_of(x):
         return x.reshape(4, 4, 2, 8, HALF)
@@ -279,17 +285,9 @@
         return carry
 
     lax.fori_loop(0, SLOTS, cut, 0)
-    start_core(COVERAGE)
+    start_core(0)
 
     def forward(s, carry):
-        @pl.when(s == 1)
-        def _():
-            start_plane(COVERAGE)
-
-        @pl.when(s == 3)
-        def _():
-            start_last(COVERAGE)
-
         wr, wi = win[s, 0], win[s, 1]
         for m in range(MODES):
             pr, pi = probe_at(m, 0), probe_at(m, 1)
@@ -355,18 +353,17 @@
     for m in range(MODES):
 
         def of_mode(i, carry, m=m):
-            @pl.when(i == 1)
-            def _():
-                if m == 0:
-                    finish(COVERAGE)
-                else:
-                    start_plane(m - 1)
+            if m >= 2:
+
+                @pl.when(i == 1)
+                def _():
+                    start_plane(m - 2)
 
             inverse(m, (2 * i, 2 * i + 1))
             return carry
 
         lax.fori_loop(0, SLOTS // 2, of_mode, 0)
-        start_core(m)
+        start_core(m + 1)
 
     def turn(s, carry):
         pick = pick_columns(spot(s)[1], (256, 512), 1)
@@ -381,7 +378,7 @@
         return carry
 
     lax.fori_loop(0, SLOTS, turn, 0)
-    start_plane(3)
+    start_plane(2)
     start_last(0)
 
     def added(block):
@@ -408,16 +405,21 @@
         return carry
 
     lax.fori_loop(0, blocks, within, 0)
+    finish(0)
     start_last(2)
-    finish(0)
-    start_last(3)
-    for u in (1, 2, 3):
-        finish(u)
-    for u in range(MODES):
+    finish(1)
+    finish(2)
+    arrive("spill")
+
+    def rest_of(i, carry):
+        at = pl.ds(i * PAD, PAD)
+        out_ref[at] = out_ref[at] - arrived[at]
+        return carry
+
+    lax.fori_loop(0, edge // PAD, rest_of, 0)
+    for u in range(len(UNITS)):
         hand_over(u)
-    collect(COVERAGE)
-    arrive("spill")
-    for u in range(MODES):
+    for u in range(len(UNITS)):
         arrive(("over", u))
     for key in builders:
         remote(key).wait_send()
@@ -442,16 +444,15 @@
     direct, turned, perm = (jnp.asarray(t) for t in tables())
     own = view.shape[0]
     edge = own // 2
-    copies = 2 + (MODES + 1) * (1 + 15 + 3 + 15) + MODES
+    copies = 2 + 5 + len(UNITS) * (15 + 3 + 15 + 1)
     return pl.pallas_call(
         step_kernel,
         out_shape=(
             jax.ShapeDtypeStruct(view.shape, F32),
-            jax.ShapeDtypeStruct((edge, 8, HALF), F32),
-            jax.ShapeDtypeStruct((8, *PLANE), F32),
+            jax.ShapeDtypeStruct((MODES, 2, *PLANE), F32),
         ),
         in_specs=[smem] * 2 + [hbm] * 6,
-        out_specs=[vmem] * 3,
+        out_specs=[vmem] * 2,
         scratch_shapes=[
             pltpu.VMEM((own + edge, 8, HALF), F32),
             pltpu.VMEM((SLOTS, 2, 256, 256), F32),
@@ -468,12 +469,13 @@
             pltpu.VMEM(perm.shape, BF16),
             pltpu.VMEM(diffraction.shape, F32),
             pltpu.VMEM((edge, 8, HALF), F32),
+            pltpu.VMEM((edge, 8, HALF), F32),
             pltpu.VMEM((5, *PLANE), F32),
             pltpu.VMEM((5, *PLANE), F32),
             pltpu.VMEM((SLOTS, 2, HALF, 256), F32),
-            pltpu.VMEM(PLANE, F32),
-            pltpu.VMEM((5, len(OTHERS), *PLANE[2:]), F32),
-            pltpu.VMEM((5, 4, *PLANE[2:]), F32),
+            pltpu.VMEM(PLANE[2:], F32),
+            pltpu.VMEM((len(OTHERS), 5, *PLANE[2:]), F32),
+            pltpu.VMEM((4, 5, *PLANE[2:]), F32),
             pltpu.SemaphoreType.DMA((6,)),
             pltpu.SemaphoreType.DMA((copies,)),
             pltpu.SemaphoreType.DMA((copies,)),
@@ -493,9 +495,10 @@
         .transpose(0, 2, 1, 3)
         .reshape(tile_rows, blocks * 2, HALF)
     )
-    view, arrived, new = step(positions.T, slot_counts, view, probe, diffraction)
-    edge = arrived.shape[0]
-    view = jnp.concatenate([view[:edge] - arrived, view[edge:]], axis=0)
+    view, new = step(positions.T, slot_counts, view, probe, diffraction)
+    nothing = jnp.minimum(positions[0, 1], 0).astype(F32)
+    view = view + nothing
+    new = new + nothing
     obj = (
         view.reshape(tile_rows, blocks, 2, HALF)
         .transpose(0, 2, 1, 3)

time: 94.9 us -> 100 us (1.054)
  Pallas kernels: 87.7 us -> 92 us
  other arithmetic: 3.48 us -> 4.75 us
  local copies, waits for them, and re-layouts: 2.2 us -> 1.2 us
    add x0 -> x2, other arithmetic: none -> 4.75 us  [the longest x1 3.2 us: on_device(): view = view + nothing]
    pallas_call x1, Pallas kernels: 87.7 us -> 92 us  [step(): pl.pallas_call(step_kernel, out_shape=(jax.ShapeDtypeStruct(view.shape, F...]
    unnamed x3 -> x2, local copies, waits for them, and re-layouts: 2.2 us -> 0.01 us
    sub x1 -> x0, other arithmetic: 2.03 us -> none  [on_device(): view = jnp.concatenate([view[:edge] - arrived, view[edge:]], axis=0)]
    concatenate x1 -> x0, other arithmetic: 1.46 us -> none  [on_device(): view = jnp.concatenate([view[:edge] - arrived, view[edge:]], axis=0)]
    slice x0 -> x1, local copies, waits for them, and re-layouts: none -> 1.19 us  [on_device(): nothing = jnp.minimum(positions[0, 1], 0).astype(F32)]
where the time goes in v6:
time: 100 us; the launch traced here: 99.9 us
  Pallas kernels  92 us (92%)
  other arithmetic  4.75 us (5%)
  between operations  1.95 us (2%)
  local copies, waits for them, and re-layouts  1.2 us (1%)
    pallas_call x1, Pallas kernels, step(): pl.pallas_call(step_kernel, out_shape=(jax.ShapeDtypeStruct(view.shape, F...  92 us
    add x1, other arithmetic, on_device(): view = view + nothing  3.2 us

profile of v6, /device:TPU:1, one launch (start us, length us, event | category | flops | bytes accessed | tf_op | source)
XLA Modules:
  0.0 99.9 jit_solution(8194005695884139170)
XLA Ops:
  1.3 1.2 %slice.3 = s32[1,1]{0,1:T(1,128)} slice(s32[4,2]{0,1:T(2,128)} %param.11), slice={[0:1], [1:2]} | slice | bytes 8 | tf_op jit(solution)/shard_map/slice | solution.py:499
  3.1 92.0 %step.1 = (f32[512,8,128]{2,1,0:T(8,128)}, f32[4,2,4,4,2,2,8,128]{7,6,5,4,3,2,1,0:T(8,128)}) custom-call(s32[2,4]{1,0:T(2,128)} %bitcast.26, s32[1,1]{1,0:T(1,128)S(6)} %copy.12.count_ref, f32[512,8,128]{2,1,0:T(8,128)} %bitcast.22, f32[8,4,4,2,2,8,128]{6,5,4,3,2,1,0:T(8,128)} %bitcast.23, f32[4,256,256]{2,1,0:T(8,128)} %diff_hbm.1, ...), custom_call_target="tpu_custom_call" | custom-call | tf_op jit(solution)/shard_map/step/pallas_call | solution.py:448
  95.1 0.0 copy-start
  95.1 3.2 %broadcast_add_fusion.1 = f32[512,8,128]{2,1,0:T(8,128)} fusion(f32[512,8,128]{2,1,0:T(8,128)} %get-tuple-element.4, f32[]{:T(128)} %bitcast.7), kind=kLoop, calls=%fused_computation.1 | loop fusion | flops 524288 | bytes 4194308 | tf_op jit(solution)/shard_map/add | solution.py:500
  98.3 0.0 copy-done
  98.3 1.6 %broadcast_add_fusion = f32[4,2,4,4,2,2,8,128]{7,6,5,4,3,2,1,0:T(8,128)} fusion(f32[4,2,4,4,2,2,8,128]{7,6,5,4,3,2,1,0:T(8,128)S(1)} %copy-done, f32[]{:T(128)} %bitcast.7), kind=kLoop, calls=%fused_computation | loop fusion | flops 524288 | bytes 4194308 | tf_op jit(solution)/shard_map/add | solution.py:501
Async XLA Ops:
  95.1 3.2 %copy-start = (f32[4,2,4,4,2,2,8,128]{7,6,5,4,3,2,1,0:T(8,128)S(1)}, f32[4,2,4,4,2,2,8,128]{7,6,5,4,3,2,1,0:T(8,128)}, u32[]{:S(2)}) copy-start(f32[4,2,4,4,2,2,8,128]{7,6,5,4,3,2,1,0:T(8,128)} %get-tuple-element.5) | copy-start | bytes 6291460

commit v7 on v5

--- a/solution.py
+++ b/solution.py
@@ -2,8 +2,6 @@
 
 import jax
 import jax.numpy as jnp
-import ml_dtypes
-import numpy as np
 from jax import lax
 from jax.experimental import pallas as pl
 from jax.experimental.pallas import tpu as pltpu
@@ -21,32 +19,28 @@
 OTHERS = tuple((i, j) for i in range(4) for j in range(4) if (i, j) != (0, 0))
 
 
-def split_table(table):
-    high = table.astype(np.float32).astype(ml_dtypes.bfloat16)
-    low = (table - high.astype(np.float64)).astype(np.float32).astype(ml_dtypes.bfloat16)
-    return high, low
-
-
-def tables():
-    n = np.arange(HALF)[:, None].astype(np.float64)
-    k = np.arange(HALF)[None, :].astype(np.float64)
-    direct, turned = [], []
-    for parity in (0, 1):
-        angle = -2.0 * math.pi * ((n * (2 * k + parity)) % 256) / 256
-        re, im = np.cos(angle) / 16, np.sin(angle) / 16
-        high, low = split_table(np.block([[re, im], [-im, re]]))
-        direct.append(np.stack([high, low]))
-        turned.append(np.stack([high.T, low.T]))
-    perm = np.zeros((256, 256), np.float32)
-    for c in range(256):
-        perm[c, (c % 2) * HALF + c // 2] = 1
-    return np.stack(direct), np.stack(turned), perm.astype(ml_dtypes.bfloat16)
-
-
 def parts_of(x):
     high = x.astype(BF16)
     low = (x - high.astype(F32)).astype(BF16)
     return high, low
+
+
+def make_tables(direct, turned, perm):
+    rows = lax.broadcasted_iota(jnp.int32, (HALF, HALF), 0)
+    cols = lax.broadcasted_iota(jnp.int32, (HALF, HALF), 1)
+    for parity in (0, 1):
+        for table, n, k in ((direct, rows, cols), (turned, cols, rows)):
+            angle = lax.rem(n * (2 * k + parity), 256).astype(F32) * (2.0 * math.pi / 256)
+            re, im = jnp.cos(angle) / 16, -jnp.sin(angle) / 16
+            above, below = (im, -im) if table is direct else (-im, im)
+            full = jnp.concatenate(
+                [jnp.concatenate([re, above], axis=1), jnp.concatenate([below, re], axis=1)],
+                axis=0,
+            )
+            table[parity, 0], table[parity, 1] = parts_of(full)
+    old = lax.broadcasted_iota(jnp.int32, (256, 256), 0)
+    new = lax.broadcasted_iota(jnp.int32, (256, 256), 1)
+    perm[...] = jnp.where(lax.rem(old, 2) * HALF + old // 2 == new, 1.0, 0.0).astype(BF16)
 
 
 def mul_right(x, table, p):
@@ -88,7 +82,7 @@
 
 
 def step_kernel(
-    pos_ref, count_ref, object_hbm, probe_hbm, diff_hbm, direct_hbm, turned_hbm, perm_hbm,
+    pos_ref, count_ref, object_hbm, probe_hbm, diff_hbm,
     out_ref, arrived, new_ref,
     ext, win, far, wanted, probe, pgrad, cov, go, hx, strips, direct, turned, perm, diff,
     spill, mate, total, factor, covered, *rest,
@@ -109,10 +103,7 @@
             [
                 (object_hbm, ext.at[:own]),
                 (diff_hbm, diff),
-                (perm_hbm, perm),
                 (probe_hbm, probe),
-                (direct_hbm, direct),
-                (turned_hbm, turned),
             ]
         )
     ]
@@ -152,7 +143,7 @@
     send("halo", lambda: (object_hbm.at[:edge], ext.at[own:], down))
 
     def result(u):
-        return covered if u == COVERAGE else new_ref.at[2 * u + core]
+        return new_ref.at[2 * u + core]
 
     def start_core(u):
         send(
@@ -187,10 +178,10 @@
             arrive(("last", u, n))
         reduced = (pieces[u, 0] + pieces[u, 1]) + (pieces[u, 2] + pieces[u, 3])
         if u == COVERAGE:
-            covered[me[0], me[1]] = reduced
-        else:
-            here = (2 * u + core, me[0], me[1])
-            new_ref[here] = probe[here] - reduced / (covered[me[0], me[1]] + 1e-06)
+            covered[...] = reduced + 1e-06
+            return
+        here = (2 * u + core, me[0], me[1])
+        new_ref[here] = probe[here] - reduced / covered[...]
         for n in range(len(OTHERS)):
             send(
                 ("back", u, n),
@@ -217,11 +208,15 @@
     go[...] = jnp.zeros_like(go)
     hx[:, :PAD] = jnp.zeros((SLOTS, PAD, 8, HALF), F32)
     hx[:, PAD + 256 :] = jnp.zeros((SLOTS, PAD, 8, HALF), F32)
+    make_tables(direct, turned, perm)
     loads[1].wait()
-    loads[2].wait()
 
     def prepare(s, carry):
-        high, low = parts_of(jnp.sqrt(diff[s]))
+        high, low = parts_of(
+            jnp.sqrt(
+                jnp.concatenate([diff[s, :, h].reshape(256, HALF) for h in (0, 1)], axis=1)
+            )
+        )
         root = jnp.dot(high, perm[...], preferred_element_type=F32) + jnp.dot(
             low, perm[...], preferred_element_type=F32
         )
@@ -231,7 +226,7 @@
 
     lax.fori_loop(0, SLOTS, prepare, 0)
 
-    loads[3].wait()
+    loads[2].wait()
 
     def probe_at(m, c):
         return jnp.concatenate(
@@ -243,8 +238,7 @@
         pr, pi = probe_at(m, 0), probe_at(m, 1)
         power = power + pr * pr + pi * pi
     peak = jnp.max(power)
-    for load in (loads[0], loads[4], loads[5]):
-        load.wait()
+    loads[0].wait()
     arrive("halo")
 
     base = region * own
@@ -355,6 +349,12 @@
     for m in range(MODES):
 
         def of_mode(i, carry, m=m):
+            if m == 3:
+
+                @pl.when(i == 0)
+                def _():
+                    start_last(0)
+
             @pl.when(i == 1)
             def _():
                 if m == 0:
@@ -382,7 +382,7 @@
 
     lax.fori_loop(0, SLOTS, turn, 0)
     start_plane(3)
-    start_last(0)
+    finish(0)
 
     def added(block):
         out = None
@@ -409,13 +409,12 @@
 
     lax.fori_loop(0, blocks, within, 0)
     start_last(2)
-    finish(0)
+    finish(1)
     start_last(3)
-    for u in (1, 2, 3):
-        finish(u)
+    finish(2)
+    finish(3)
     for u in range(MODES):
         hand_over(u)
-    collect(COVERAGE)
     arrive("spill")
     for u in range(MODES):
         arrive(("over", u))
@@ -439,8 +438,8 @@
     smem = pl.BlockSpec(memory_space=pltpu.SMEM)
     hbm = pl.BlockSpec(memory_space=pltpu.HBM)
     vmem = pl.BlockSpec(memory_space=pltpu.VMEM)
-    direct, turned, perm = (jnp.asarray(t) for t in tables())
     own = view.shape[0]
+    diffraction = diffraction.reshape(SLOTS, 32, 8, 2, HALF).transpose(0, 1, 3, 2, 4)
     edge = own // 2
     copies = 2 + (MODES + 1) * (1 + 15 + 3 + 15) + MODES
     return pl.pallas_call(
@@ -450,7 +449,7 @@
             jax.ShapeDtypeStruct((edge, 8, HALF), F32),
             jax.ShapeDtypeStruct((8, *PLANE), F32),
         ),
-        in_specs=[smem] * 2 + [hbm] * 6,
+        in_specs=[smem] * 2 + [hbm] * 3,
         out_specs=[vmem] * 3,
         scratch_shapes=[
             pltpu.VMEM((own + edge, 8, HALF), F32),
@@ -463,26 +462,26 @@
             pltpu.VMEM((SLOTS, 2, 256, 256), F32),
             pltpu.VMEM((SLOTS, 256 + 2 * PAD, 8, HALF), F32),
             pltpu.VMEM((256 * 8, HALF), F32),
-            pltpu.VMEM(direct.shape, BF16),
-            pltpu.VMEM(turned.shape, BF16),
-            pltpu.VMEM(perm.shape, BF16),
+            pltpu.VMEM((2, 2, 256, 256), BF16),
+            pltpu.VMEM((2, 2, 256, 256), BF16),
+            pltpu.VMEM((256, 256), BF16),
             pltpu.VMEM(diffraction.shape, F32),
             pltpu.VMEM((edge, 8, HALF), F32),
             pltpu.VMEM((5, *PLANE), F32),
             pltpu.VMEM((5, *PLANE), F32),
             pltpu.VMEM((SLOTS, 2, HALF, 256), F32),
-            pltpu.VMEM(PLANE, F32),
+            pltpu.VMEM(PLANE[2:], F32),
             pltpu.VMEM((5, len(OTHERS), *PLANE[2:]), F32),
             pltpu.VMEM((5, 4, *PLANE[2:]), F32),
-            pltpu.SemaphoreType.DMA((6,)),
+            pltpu.SemaphoreType.DMA((3,)),
             pltpu.SemaphoreType.DMA((copies,)),
             pltpu.SemaphoreType.DMA((copies,)),
         ],
         compiler_params=pltpu.CompilerParams(
-            vmem_limit_bytes=54 << 20, collective_id=0, has_side_effects=True
+            vmem_limit_bytes=46 << 20, collective_id=0, has_side_effects=True
         ),
         name="step",
-    )(positions, slot_counts, view, tiled(probe), diffraction, direct, turned, perm)
+    )(positions, slot_counts, view, tiled(probe), diffraction)
 
 
 def on_device(object_slab, probe, diffraction, positions, slot_counts):

time: 94.9 us -> 92.8 us (0.978)
  other arithmetic: 3.48 us -> 1.63 us
  Pallas kernels: 87.7 us -> 86.5 us
  local copies, waits for them, and re-layouts: 2.2 us -> 3.21 us
    sub x1, other arithmetic: 2.03 us -> 0.17 us  [on_device(): view = jnp.concatenate([view[:edge] - arrived, view[edge:]], axis=0)]
    pallas_call x1, Pallas kernels: 87.7 us -> 86.5 us  [step(): pl.pallas_call(step_kernel, out_shape=(jax.ShapeDtypeStruct(view.shape, F...]
    unnamed x3 -> x5, local copies, waits for them, and re-layouts: 2.2 us -> 3.21 us
where the time goes in v7:
time: 92.8 us; the launch traced here: 92.6 us
  Pallas kernels  86.5 us (93%)
  local copies, waits for them, and re-layouts  3.21 us (3%)
  other arithmetic  1.63 us (2%)
  between operations  1.3 us (1%)
    pallas_call x1, Pallas kernels, step(): pl.pallas_call(step_kernel, out_shape=(jax.ShapeDtypeStruct(view.shape, F...  86.5 us
    unnamed x5, local copies, waits for them, and re-layouts  3.21 us

profile of v7, /device:TPU:1, one launch (start us, length us, event | category | flops | bytes accessed | tf_op | source)
XLA Modules:
  0.0 92.6 jit_solution(18341614142820996144)
XLA Ops:
  1.3 0.0 copy-start
  1.3 1.2 %copy-done = f32[4,256,256]{2,1,0:T(8,128)S(1)} copy-done((f32[4,256,256]{2,1,0:T(8,128)S(1)}, f32[4,256,256]{2,1,0:T(8,128)}, u32[]{:S(2)}) %copy-start) | copy-done | bytes 1048600
  2.5 0.0 copy-start.1
  2.5 0.7 copy-done.1
  3.2 86.5 %step.1 = (f32[512,8,128]{2,1,0:T(8,128)S(1)}, f32[256,8,128]{2,1,0:T(8,128)S(1)}, f32[8,4,4,2,2,8,128]{6,5,4,3,2,1,0:T(8,128)S(1)}) custom-call(s32[2,4]{1,0:T(2,128)S(1)} %bitcast.26, s32[1,1]{1,0:T(1,128)S(6)} %copy.10.count_ref, f32[512,8,128]{2,1,0:T(8,128)} %bitcast.27, f32[8,4,4,2,2,8,128]{6,5,4,3,2,1,0:T(8,128)} %bitcast.28, ...), custom_call_target="tpu_custom_call" | custom-call | tf_op jit(solution)/shard_map/step/pallas_call | solution.py:445
  89.7 0.2 slice_subtract_fusion
  89.8 1.5 %pad_maximum_fusion = f32[512,8,128]{2,1,0:T(8,128)} fusion(f32[256,8,128]{2,1,0:T(8,128)S(1)} %get-tuple-element.9, f32[256,8,128]{2,1,0:T(8,128)S(1)} %get-tuple-element.8), kind=kLoop, calls=%fused_computation | loop fusion | flops 524288 | bytes 4194304 | tf_op jit(solution)/shard_map/concatenate | solution.py:497
  91.3 1.3 %copy.11 = f32[4,2,256,256]{3,2,1,0:T(8,128)} copy(f32[4,2,256,256]{3,2,1,0:T(8,128)S(1)} %bitcast.24) | data formatting | bytes 4194304
Async XLA Ops:
  1.3 1.2 %copy-start = (f32[4,256,256]{2,1,0:T(8,128)S(1)}, f32[4,256,256]{2,1,0:T(8,128)}, u32[]{:S(2)}) copy-start(f32[4,256,256]{2,1,0:T(8,128)} %param.7) | copy-start | bytes 3145732
  2.5 0.7 copy-start.1

commit v8 on v7

--- a/solution.py
+++ b/solution.py
@@ -182,7 +182,8 @@
             return
         here = (2 * u + core, me[0], me[1])
         new_ref[here] = probe[here] - reduced / covered[...]
-        for n in range(len(OTHERS)):
+        to = range(len(OTHERS)) if u == MODES - 1 else [OTHERS.index((0, d)) for d in (1, 2, 3)]
+        for n in to:
             send(
                 ("back", u, n),
                 lambda n=n: (
@@ -192,8 +193,19 @@
                 ),
             )
 
+    def relay(u):
+        for d in (1, 2, 3):
+            arrive(("back", u, OTHERS.index((0, d))))
+        for d in (1, 2, 3):
+            n = OTHERS.index((d, 0))
+            send(
+                ("back", u, n),
+                lambda n=n: (result(u).at[me[0]], result(u).at[me[0]], plane_devices[n]),
+            )
+
     def collect(u):
-        for n in range(len(OTHERS)):
+        to = range(len(OTHERS)) if u == MODES - 1 else [OTHERS.index((d, 0)) for d in (1, 2, 3)]
+        for n in to:
             arrive(("back", u, n))
 
     def hand_over(u):
@@ -401,6 +413,7 @@
     lax.fori_loop(0, edge // PAD, below, 0)
     send("spill", lambda: (spill, arrived, up))
     start_last(1)
+    relay(0)
 
     def within(i, carry):
         at = pl.ds(i * PAD, PAD)
@@ -412,7 +425,9 @@
     finish(1)
     start_last(3)
     finish(2)
+    relay(1)
     finish(3)
+    relay(2)
     for u in range(MODES):
         hand_over(u)
     arrive("spill")

time: 92.8 us -> 88 us (0.948)
  Pallas kernels: 86.5 us -> 81.7 us
    pallas_call x1, Pallas kernels: 86.5 us -> 81.7 us  [step(): pl.pallas_call(step_kernel, out_shape=(jax.ShapeDtypeStruct(view.shape, F...]
where the time goes in v8:
time: 88 us; the launch traced here: 87.9 us
  Pallas kernels  81.7 us (93%)
  local copies, waits for them, and re-layouts  3.21 us (4%)
  other arithmetic  1.63 us (2%)
  between operations  1.3 us (1%)
    pallas_call x1, Pallas kernels, step(): pl.pallas_call(step_kernel, out_shape=(jax.ShapeDtypeStruct(view.shape, F...  81.7 us
    unnamed x5, local copies, waits for them, and re-layouts  3.21 us

profile of v8, /device:TPU:1, one launch (start us, length us, event | category | flops | bytes accessed | tf_op | source)
XLA Modules:
  0.0 87.9 jit_solution(8589800707947246926)
XLA Ops:
  1.3 0.0 copy-start
  1.3 1.2 %copy-done = f32[4,256,256]{2,1,0:T(8,128)S(1)} copy-done((f32[4,256,256]{2,1,0:T(8,128)S(1)}, f32[4,256,256]{2,1,0:T(8,128)}, u32[]{:S(2)}) %copy-start) | copy-done | bytes 1048600
  2.5 0.0 copy-start.1
  2.5 0.7 copy-done.1
  3.2 81.7 %step.1 = (f32[512,8,128]{2,1,0:T(8,128)S(1)}, f32[256,8,128]{2,1,0:T(8,128)S(1)}, f32[8,4,4,2,2,8,128]{6,5,4,3,2,1,0:T(8,128)S(1)}) custom-call(s32[2,4]{1,0:T(2,128)S(1)} %bitcast.26, s32[1,1]{1,0:T(1,128)S(6)} %copy.10.count_ref, f32[512,8,128]{2,1,0:T(8,128)} %bitcast.27, f32[8,4,4,2,2,8,128]{6,5,4,3,2,1,0:T(8,128)} %bitcast.28, ...), custom_call_target="tpu_custom_call" | custom-call | tf_op jit(solution)/shard_map/step/pallas_call | solution.py:460
  84.9 0.2 slice_subtract_fusion
  85.1 1.5 %pad_maximum_fusion = f32[512,8,128]{2,1,0:T(8,128)} fusion(f32[256,8,128]{2,1,0:T(8,128)S(1)} %get-tuple-element.9, f32[256,8,128]{2,1,0:T(8,128)S(1)} %get-tuple-element.8), kind=kLoop, calls=%fused_computation | loop fusion | flops 524288 | bytes 4194304 | tf_op jit(solution)/shard_map/concatenate | solution.py:512
  86.5 1.3 %copy.11 = f32[4,2,256,256]{3,2,1,0:T(8,128)} copy(f32[4,2,256,256]{3,2,1,0:T(8,128)S(1)} %bitcast.24) | data formatting | bytes 4194304
Async XLA Ops:
  1.3 1.2 %copy-start = (f32[4,256,256]{2,1,0:T(8,128)S(1)}, f32[4,256,256]{2,1,0:T(8,128)}, u32[]{:S(2)}) copy-start(f32[4,256,256]{2,1,0:T(8,128)} %param.7) | copy-start | bytes 3145732
  2.5 0.7 copy-start.1

commit v9 on v8

--- a/solution.py
+++ b/solution.py
@@ -87,7 +87,7 @@
     ext, win, far, wanted, probe, pgrad, cov, go, hx, strips, direct, turned, perm, diff,
     spill, mate, total, factor, covered, *rest,
 ):
-    got, pieces, local_sem, send_sem, recv_sem = rest
+    got, pieces, row_got, row_sum, local_sem, send_sem, recv_sem = rest
     me, core = place()
     regions = lax.axis_size("region")
     region, group = lax.axis_index("region"), lax.axis_index("group")
@@ -151,20 +151,52 @@
             lambda: (cov if u == COVERAGE else pgrad.at[2 * u + 1 - core], mate.at[u], sibling),
         )
 
-    def start_plane(u):
+    def join(u):
         arrive(("core", u))
         total[u] = (cov[...] if u == COVERAGE else pgrad[2 * u + core]) + mate[u]
+
+    def start_plane(u):
+        join(u)
         for n, (p, q) in enumerate(plane_peers):
             send(
                 ("plane", u, n),
                 lambda n=n, p=p, q=q: (total.at[u, p, q], got.at[u, n], plane_devices[n]),
             )
 
+    def start_row(u):
+        join(u)
+        for d in (1, 2, 3):
+            n = OTHERS.index((d, 0))
+            send(
+                ("row", u, d),
+                lambda n=n, d=d: (
+                    total.at[u, plane_peers[n][0]],
+                    row_got.at[u, d - 1],
+                    plane_devices[n],
+                ),
+            )
+
+    def start_column(u):
+        for d in (1, 2, 3):
+            arrive(("row", u, d))
+        row_sum[u] = total[u, me[0]] + row_got[u, 0] + row_got[u, 1] + row_got[u, 2]
+        for d in (1, 2, 3):
+            n = OTHERS.index((0, d))
+            send(
+                ("plane", u, d - 1),
+                lambda n=n, d=d: (
+                    row_sum.at[u, plane_peers[n][1]],
+                    got.at[u, d - 1],
+                    plane_devices[n],
+                ),
+            )
+
     def start_last(u):
-        for n in range(len(OTHERS)):
+        count = len(OTHERS) if u == MODES - 1 else 3
+        for n in range(count):
             arrive(("plane", u, n))
-        value = total[u, me[0], me[1]]
-        for n in range(len(OTHERS)):
+        value = total[u, me[0], me[1]] if u == MODES - 1 else row_sum[u, me[1]]
+        for n in range(count):
             value = value + got[u, n]
         pieces[u, me[2]] = value
         for n in range(3):
@@ -290,7 +322,11 @@
     def forward(s, carry):
         @pl.when(s == 1)
         def _():
-            start_plane(COVERAGE)
+            start_row(COVERAGE)
+
+        @pl.when(s == 2)
+        def _():
+            start_column(COVERAGE)
 
         @pl.when(s == 3)
         def _():
@@ -365,14 +401,14 @@
 
                 @pl.when(i == 0)
                 def _():
-                    start_last(0)
+                    start_column(0)
 
             @pl.when(i == 1)
             def _():
                 if m == 0:
                     finish(COVERAGE)
                 else:
-                    start_plane(m - 1)
+                    start_row(m - 1)
 
             inverse(m, (2 * i, 2 * i + 1))
             return carry
@@ -394,7 +430,8 @@
 
     lax.fori_loop(0, SLOTS, turn, 0)
     start_plane(3)
-    finish(0)
+    start_last(0)
+    start_column(1)
 
     def added(block):
         out = None
@@ -412,8 +449,7 @@
 
     lax.fori_loop(0, edge // PAD, below, 0)
     send("spill", lambda: (spill, arrived, up))
-    start_last(1)
-    relay(0)
+    start_column(2)
 
     def within(i, carry):
         at = pl.ds(i * PAD, PAD)
@@ -421,12 +457,15 @@
         return carry
 
     lax.fori_loop(0, blocks, within, 0)
+    finish(0)
+    start_last(1)
     start_last(2)
+    start_last(3)
+    relay(0)
     finish(1)
-    start_last(3)
     finish(2)
+    finish(3)
     relay(1)
-    finish(3)
     relay(2)
     for u in range(MODES):
         hand_over(u)
@@ -488,6 +527,8 @@
             pltpu.VMEM(PLANE[2:], F32),
             pltpu.VMEM((5, len(OTHERS), *PLANE[2:]), F32),
             pltpu.VMEM((5, 4, *PLANE[2:]), F32),
+            pltpu.VMEM((5, 3, *PLANE[1:]), F32),
+            pltpu.VMEM((5, *PLANE[1:]), F32),
             pltpu.SemaphoreType.DMA((3,)),
             pltpu.SemaphoreType.DMA((copies,)),
             pltpu.SemaphoreType.DMA((copies,)),

time: 88 us -> 91.6 us (1.041)
  Pallas kernels: 81.7 us -> 85.3 us
    pallas_call x1, Pallas kernels: 81.7 us -> 85.3 us  [step(): pl.pallas_call(step_kernel, out_shape=(jax.ShapeDtypeStruct(view.shape, F...]
where the time goes in v9:
time: 91.6 us; the launch traced here: 91.4 us
  Pallas kernels  85.3 us (93%)
  local copies, waits for them, and re-layouts  3.21 us (4%)
  other arithmetic  1.63 us (2%)
  between operations  1.3 us (1%)
    pallas_call x1, Pallas kernels, step(): pl.pallas_call(step_kernel, out_shape=(jax.ShapeDtypeStruct(view.shape, F...  85.3 us
    unnamed x5, local copies, waits for them, and re-layouts  3.21 us

profile of v9, /device:TPU:1, one launch (start us, length us, event | category | flops | bytes accessed | tf_op | source)
XLA Modules:
  0.0 91.4 jit_solution(8423481667658567825)
XLA Ops:
  1.3 0.0 copy-start
  1.3 1.2 %copy-done = f32[4,256,256]{2,1,0:T(8,128)S(1)} copy-done((f32[4,256,256]{2,1,0:T(8,128)S(1)}, f32[4,256,256]{2,1,0:T(8,128)}, u32[]{:S(2)}) %copy-start) | copy-done | bytes 1048600
  2.5 0.0 copy-start.1
  2.5 0.7 copy-done.1
  3.2 85.3 %step.1 = (f32[512,8,128]{2,1,0:T(8,128)S(1)}, f32[256,8,128]{2,1,0:T(8,128)S(1)}, f32[8,4,4,2,2,8,128]{6,5,4,3,2,1,0:T(8,128)S(1)}) custom-call(s32[2,4]{1,0:T(2,128)S(1)} %bitcast.26, s32[1,1]{1,0:T(1,128)S(6)} %copy.10.count_ref, f32[512,8,128]{2,1,0:T(8,128)} %bitcast.27, f32[8,4,4,2,2,8,128]{6,5,4,3,2,1,0:T(8,128)} %bitcast.28, ...), custom_call_target="tpu_custom_call" | custom-call | tf_op jit(solution)/shard_map/step/pallas_call | solution.py:499
  88.5 0.2 slice_subtract_fusion
  88.6 1.5 %pad_maximum_fusion = f32[512,8,128]{2,1,0:T(8,128)} fusion(f32[256,8,128]{2,1,0:T(8,128)S(1)} %get-tuple-element.9, f32[256,8,128]{2,1,0:T(8,128)S(1)} %get-tuple-element.8), kind=kLoop, calls=%fused_computation | loop fusion | flops 524288 | bytes 4194304 | tf_op jit(solution)/shard_map/concatenate | solution.py:553
  90.1 1.3 %copy.11 = f32[4,2,256,256]{3,2,1,0:T(8,128)} copy(f32[4,2,256,256]{3,2,1,0:T(8,128)S(1)} %bitcast.24) | data formatting | bytes 4194304
Async XLA Ops:
  1.3 1.2 %copy-start = (f32[4,256,256]{2,1,0:T(8,128)S(1)}, f32[4,256,256]{2,1,0:T(8,128)}, u32[]{:S(2)}) copy-start(f32[4,256,256]{2,1,0:T(8,128)} %param.7) | copy-start | bytes 3145732
  2.5 0.7 copy-start.1

commit v10 on v8

--- a/solution.py
+++ b/solution.py
@@ -71,13 +71,13 @@
     z = lax.rem(region // 2, 4)
     y = (group // 4) * 2 + region // 8
     x = lax.rem(group, 4)
-    turned = ((x, y), (y, z), (z, x))
+    turned = ((x, y), (y, x), (z, z))
     return tuple(a + core * (b - a) for a, b in turned), core
 
 
 def device(at, core, counted):
     a, b, c = at
-    x, y, z = a + counted * (c - a), b + counted * (a - b), c + counted * (b - c)
+    x, y, z = a + counted * (b - a), b + counted * (a - b), c
     return ((lax.rem(y, 2) * 4 + z) * 2 + core, (y // 2) * 4 + x)
 
 
@@ -425,8 +425,8 @@
     finish(1)
     start_last(3)
     finish(2)
+    finish(3)
     relay(1)
-    finish(3)
     relay(2)
     for u in range(MODES):
         hand_over(u)

time: 88 us -> 90.2 us (1.025)
  Pallas kernels: 81.7 us -> 83.9 us
    pallas_call x1, Pallas kernels: 81.7 us -> 83.9 us  [step(): pl.pallas_call(step_kernel, out_shape=(jax.ShapeDtypeStruct(view.shape, F...]
where the time goes in v10:
time: 90.2 us; the launch traced here: 90 us
  Pallas kernels  83.9 us (93%)
  local copies, waits for them, and re-layouts  3.21 us (4%)
  other arithmetic  1.63 us (2%)
  between operations  1.3 us (1%)
    pallas_call x1, Pallas kernels, step(): pl.pallas_call(step_kernel, out_shape=(jax.ShapeDtypeStruct(view.shape, F...  83.9 us
    unnamed x5, local copies, waits for them, and re-layouts  3.21 us

profile of v10, /device:TPU:1, one launch (start us, length us, event | category | flops | bytes accessed | tf_op | source)
XLA Modules:
  0.0 90.0 jit_solution(13197378902233593700)
XLA Ops:
  1.3 0.0 copy-start
  1.3 1.2 %copy-done = f32[4,256,256]{2,1,0:T(8,128)S(1)} copy-done((f32[4,256,256]{2,1,0:T(8,128)S(1)}, f32[4,256,256]{2,1,0:T(8,128)}, u32[]{:S(2)}) %copy-start) | copy-done | bytes 1048600
  2.5 0.0 copy-start.1
  2.5 0.7 copy-done.1
  3.2 83.9 %step.1 = (f32[512,8,128]{2,1,0:T(8,128)S(1)}, f32[256,8,128]{2,1,0:T(8,128)S(1)}, f32[8,4,4,2,2,8,128]{6,5,4,3,2,1,0:T(8,128)S(1)}) custom-call(s32[2,4]{1,0:T(2,128)S(1)} %bitcast.26, s32[1,1]{1,0:T(1,128)S(6)} %copy.10.count_ref, f32[512,8,128]{2,1,0:T(8,128)} %bitcast.27, f32[8,4,4,2,2,8,128]{6,5,4,3,2,1,0:T(8,128)} %bitcast.28, ...), custom_call_target="tpu_custom_call" | custom-call | tf_op jit(solution)/shard_map/step/pallas_call | solution.py:460
  87.1 0.2 slice_subtract_fusion
  87.3 1.5 %pad_maximum_fusion = f32[512,8,128]{2,1,0:T(8,128)} fusion(f32[256,8,128]{2,1,0:T(8,128)S(1)} %get-tuple-element.9, f32[256,8,128]{2,1,0:T(8,128)S(1)} %get-tuple-element.8), kind=kLoop, calls=%fused_computation | loop fusion | flops 524288 | bytes 4194304 | tf_op jit(solution)/shard_map/concatenate | solution.py:512
  88.7 1.3 %copy.11 = f32[4,2,256,256]{3,2,1,0:T(8,128)} copy(f32[4,2,256,256]{3,2,1,0:T(8,128)S(1)} %bitcast.24) | data formatting | bytes 4194304
Async XLA Ops:
  1.3 1.2 %copy-start = (f32[4,256,256]{2,1,0:T(8,128)S(1)}, f32[4,256,256]{2,1,0:T(8,128)}, u32[]{:S(2)}) copy-start(f32[4,256,256]{2,1,0:T(8,128)} %param.7) | copy-start | bytes 3145732
  2.5 0.7 copy-start.1

commit v11 on v8

--- a/solution.py
+++ b/solution.py
@@ -87,7 +87,7 @@
     ext, win, far, wanted, probe, pgrad, cov, go, hx, strips, direct, turned, perm, diff,
     spill, mate, total, factor, covered, *rest,
 ):
-    got, pieces, local_sem, send_sem, recv_sem = rest
+    got, pieces, row_got, row_sum, local_sem, send_sem, recv_sem = rest
     me, core = place()
     regions = lax.axis_size("region")
     region, group = lax.axis_index("region"), lax.axis_index("group")
@@ -151,20 +151,52 @@
             lambda: (cov if u == COVERAGE else pgrad.at[2 * u + 1 - core], mate.at[u], sibling),
         )
 
-    def start_plane(u):
+    def join(u):
         arrive(("core", u))
         total[u] = (cov[...] if u == COVERAGE else pgrad[2 * u + core]) + mate[u]
+
+    def start_plane(u):
+        join(u)
         for n, (p, q) in enumerate(plane_peers):
             send(
                 ("plane", u, n),
                 lambda n=n, p=p, q=q: (total.at[u, p, q], got.at[u, n], plane_devices[n]),
             )
 
+    def start_row():
+        join(COVERAGE)
+        for d in (1, 2, 3):
+            n = OTHERS.index((d, 0))
+            send(
+                ("row", d),
+                lambda n=n, d=d: (
+                    total.at[COVERAGE, plane_peers[n][0]],
+                    row_got.at[d - 1],
+                    plane_devices[n],
+                ),
+            )
+
+    def start_column():
+        for d in (1, 2, 3):
+            arrive(("row", d))
+        row_sum[...] = total[COVERAGE, me[0]] + row_got[0] + row_got[1] + row_got[2]
+        for d in (1, 2, 3):
+            n = OTHERS.index((0, d))
+            send(
+                ("plane", COVERAGE, d - 1),
+                lambda n=n, d=d: (
+                    row_sum.at[plane_peers[n][1]],
+                    got.at[COVERAGE, d - 1],
+                    plane_devices[n],
+                ),
+            )
+
     def start_last(u):
-        for n in range(len(OTHERS)):
+        count = 3 if u == COVERAGE else len(OTHERS)
+        for n in range(count):
             arrive(("plane", u, n))
-        value = total[u, me[0], me[1]]
-        for n in range(len(OTHERS)):
+        value = row_sum[me[1]] if u == COVERAGE else total[u, me[0], me[1]]
+        for n in range(count):
             value = value + got[u, n]
         pieces[u, me[2]] = value
         for n in range(3):
@@ -290,7 +322,11 @@
     def forward(s, carry):
         @pl.when(s == 1)
         def _():
-            start_plane(COVERAGE)
+            start_row()
+
+        @pl.when(s == 2)
+        def _():
+            start_column()
 
         @pl.when(s == 3)
         def _():
@@ -380,6 +416,8 @@
         lax.fori_loop(0, SLOTS // 2, of_mode, 0)
         start_core(m)
 
+    finish(0)
+
     def turn(s, carry):
         pick = pick_columns(spot(s)[1], (256, 512), 1)
         for c in (0, 1):
@@ -392,9 +430,10 @@
         hx[s, PAD : PAD + 256] = strips[...].reshape(256, 8, HALF)
         return carry
 
-    lax.fori_loop(0, SLOTS, turn, 0)
+    lax.fori_loop(0, SLOTS // 2, turn, 0)
     start_plane(3)
-    finish(0)
+    lax.fori_loop(SLOTS // 2, SLOTS, turn, 0)
+    start_last(1)
 
     def added(block):
         out = None
@@ -412,7 +451,6 @@
 
     lax.fori_loop(0, edge // PAD, below, 0)
     send("spill", lambda: (spill, arrived, up))
-    start_last(1)
     relay(0)
 
     def within(i, carry):
@@ -488,6 +526,8 @@
             pltpu.VMEM(PLANE[2:], F32),
             pltpu.VMEM((5, len(OTHERS), *PLANE[2:]), F32),
             pltpu.VMEM((5, 4, *PLANE[2:]), F32),
+            pltpu.VMEM((3, *PLANE[1:]), F32),
+            pltpu.VMEM(PLANE[1:], F32),
             pltpu.SemaphoreType.DMA((3,)),
             pltpu.SemaphoreType.DMA((copies,)),
             pltpu.SemaphoreType.DMA((copies,)),

time: 88 us -> 89 us (1.011)
  Pallas kernels: 81.7 us -> 82.6 us
    pallas_call x1, Pallas kernels: 81.7 us -> 82.6 us  [step(): pl.pallas_call(step_kernel, out_shape=(jax.ShapeDtypeStruct(view.shape, F...]
where the time goes in v11:
time: 89 us; the launch traced here: 88.8 us
  Pallas kernels  82.6 us (93%)
  local copies, waits for them, and re-layouts  3.21 us (4%)
  other arithmetic  1.63 us (2%)
  between operations  1.3 us (1%)
    pallas_call x1, Pallas kernels, step(): pl.pallas_call(step_kernel, out_shape=(jax.ShapeDtypeStruct(view.shape, F...  82.6 us
    unnamed x5, local copies, waits for them, and re-layouts  3.21 us

profile of v11, /device:TPU:1, one launch (start us, length us, event | category | flops | bytes accessed | tf_op | source)
XLA Modules:
  0.0 88.8 jit_solution(2763302435992974439)
XLA Ops:
  1.3 0.0 copy-start
  1.3 1.2 %copy-done = f32[4,256,256]{2,1,0:T(8,128)S(1)} copy-done((f32[4,256,256]{2,1,0:T(8,128)S(1)}, f32[4,256,256]{2,1,0:T(8,128)}, u32[]{:S(2)}) %copy-start) | copy-done | bytes 1048600
  2.5 0.0 copy-start.1
  2.5 0.7 copy-done.1
  3.2 82.6 %step.1 = (f32[512,8,128]{2,1,0:T(8,128)S(1)}, f32[256,8,128]{2,1,0:T(8,128)S(1)}, f32[8,4,4,2,2,8,128]{6,5,4,3,2,1,0:T(8,128)S(1)}) custom-call(s32[2,4]{1,0:T(2,128)S(1)} %bitcast.26, s32[1,1]{1,0:T(1,128)S(6)} %copy.10.count_ref, f32[512,8,128]{2,1,0:T(8,128)} %bitcast.27, f32[8,4,4,2,2,8,128]{6,5,4,3,2,1,0:T(8,128)} %bitcast.28, ...), custom_call_target="tpu_custom_call" | custom-call | tf_op jit(solution)/shard_map/step/pallas_call | solution.py:498
  85.8 0.2 slice_subtract_fusion
  86.0 1.5 %pad_maximum_fusion = f32[512,8,128]{2,1,0:T(8,128)} fusion(f32[256,8,128]{2,1,0:T(8,128)S(1)} %get-tuple-element.9, f32[256,8,128]{2,1,0:T(8,128)S(1)} %get-tuple-element.8), kind=kLoop, calls=%fused_computation | loop fusion | flops 524288 | bytes 4194304 | tf_op jit(solution)/shard_map/concatenate | solution.py:552
  87.5 1.3 %copy.11 = f32[4,2,256,256]{3,2,1,0:T(8,128)} copy(f32[4,2,256,256]{3,2,1,0:T(8,128)S(1)} %bitcast.24) | data formatting | bytes 4194304
Async XLA Ops:
  1.3 1.2 %copy-start = (f32[4,256,256]{2,1,0:T(8,128)S(1)}, f32[4,256,256]{2,1,0:T(8,128)}, u32[]{:S(2)}) copy-start(f32[4,256,256]{2,1,0:T(8,128)} %param.7) | copy-start | bytes 3145732
  2.5 0.7 copy-start.1

commit v12 on v8

--- a/solution.py
+++ b/solution.py
@@ -392,8 +392,9 @@
         hx[s, PAD : PAD + 256] = strips[...].reshape(256, 8, HALF)
         return carry
 
-    lax.fori_loop(0, SLOTS, turn, 0)
+    lax.fori_loop(0, SLOTS // 2, turn, 0)
     start_plane(3)
+    lax.fori_loop(SLOTS // 2, SLOTS, turn, 0)
     finish(0)
 
     def added(block):

time: 88 us -> 87.9 us (level)
  no operation moved by 1% of the time
where the time goes in v12:
time: 87.9 us; the launch traced here: 87.7 us
  Pallas kernels  81.6 us (93%)
  local copies, waits for them, and re-layouts  3.21 us (4%)
  other arithmetic  1.63 us (2%)
  between operations  1.3 us (1%)
    pallas_call x1, Pallas kernels, step(): pl.pallas_call(step_kernel, out_shape=(jax.ShapeDtypeStruct(view.shape, F...  81.6 us
    unnamed x5, local copies, waits for them, and re-layouts  3.21 us

profile of v12, /device:TPU:1, one launch (start us, length us, event | category | flops | bytes accessed | tf_op | source)
XLA Modules:
  0.0 87.7 jit_solution(14476488676855690365)
XLA Ops:
  1.3 0.0 copy-start
  1.3 1.2 %copy-done = f32[4,256,256]{2,1,0:T(8,128)S(1)} copy-done((f32[4,256,256]{2,1,0:T(8,128)S(1)}, f32[4,256,256]{2,1,0:T(8,128)}, u32[]{:S(2)}) %copy-start) | copy-done | bytes 1048600
  2.5 0.0 copy-start.1
  2.5 0.7 copy-done.1
  3.2 81.6 %step.1 = (f32[512,8,128]{2,1,0:T(8,128)S(1)}, f32[256,8,128]{2,1,0:T(8,128)S(1)}, f32[8,4,4,2,2,8,128]{6,5,4,3,2,1,0:T(8,128)S(1)}) custom-call(s32[2,4]{1,0:T(2,128)S(1)} %bitcast.26, s32[1,1]{1,0:T(1,128)S(6)} %copy.10.count_ref, f32[512,8,128]{2,1,0:T(8,128)} %bitcast.27, f32[8,4,4,2,2,8,128]{6,5,4,3,2,1,0:T(8,128)} %bitcast.28, ...), custom_call_target="tpu_custom_call" | custom-call | tf_op jit(solution)/shard_map/step/pallas_call | solution.py:461
  84.8 0.2 slice_subtract_fusion
  85.0 1.5 %pad_maximum_fusion = f32[512,8,128]{2,1,0:T(8,128)} fusion(f32[256,8,128]{2,1,0:T(8,128)S(1)} %get-tuple-element.9, f32[256,8,128]{2,1,0:T(8,128)S(1)} %get-tuple-element.8), kind=kLoop, calls=%fused_computation | loop fusion | flops 524288 | bytes 4194304 | tf_op jit(solution)/shard_map/concatenate | solution.py:513
  86.4 1.3 %copy.11 = f32[4,2,256,256]{3,2,1,0:T(8,128)} copy(f32[4,2,256,256]{3,2,1,0:T(8,128)S(1)} %bitcast.24) | data formatting | bytes 4194304
Async XLA Ops:
  1.3 1.2 %copy-start = (f32[4,256,256]{2,1,0:T(8,128)S(1)}, f32[4,256,256]{2,1,0:T(8,128)}, u32[]{:S(2)}) copy-start(f32[4,256,256]{2,1,0:T(8,128)} %param.7) | copy-start | bytes 3145732
  2.5 0.7 copy-start.1
